TPU v7x, 512 devices: a whole 4x8x8 slice. The times are simulated.
512 devices in a mesh: ctx: 64 (over y, z_lo, x), mp: 8 (over z_hi, core).
Axes of the slice: x: 4, y: 8, z: 8 (z_hi: 4, z_lo: 2; z = z_hi * 2 + z_lo), core: 2. Of those that a mesh axis runs over, the one named last changes fastest.
Arguments:
- queries: bfloat16 [16384, 8192], P('ctx', 'mp'), may hold values from -6 to 6
- key_feats: bfloat16 [16384, 8192], P('ctx', 'mp'), may hold values from -6 to 6
- value_feats: bfloat16 [16384, 8192], P('ctx', 'mp'), may hold values from -6 to 6
- filters: bfloat16 [512, 128], P('mp'), may hold values from -0.5 to 0.5
- grad_out: bfloat16 [16384, 8192], P('ctx', 'mp'), may hold values from -40 to 40
Outputs:
- mixer_out: bfloat16 [16384, 8192], P('ctx', 'mp')
- grad_queries: bfloat16 [16384, 8192], P('ctx', 'mp')
- grad_keys: bfloat16 [16384, 8192], P('ctx', 'mp')
- grad_values: bfloat16 [16384, 8192], P('ctx', 'mp')
- grad_filters: float32 [512, 128], P('mp')
All inputs are finite; a program needn't handle non-finite values.
Results may differ from a plain program's by a relative error of at most 0.0058.
Values may be sent and summed in bfloat16 or wider, within the bound.
No kernel may reach another device: no remote copies, remote signals or barrier semaphores. Data moves between devices by JAX's collectives and lax.ppermute only.
A program may use at most 64 MiB of HBM per device.

v0:
```python
import jax
import jax.numpy as jnp
from jax import lax
from jax.sharding import PartitionSpec as P

D = 8192
G = 16


def contract(formula, first_op, second_op):
    return jnp.einsum(formula, first_op, second_op, preferred_element_type=jnp.float32)


def toeplitz(filt):
    count, filter_len = filt.shape
    flipped = filt[:, ::-1]
    lead_zero = jnp.zeros((count, 1), filt.dtype)
    trailing = jnp.zeros((count, filter_len), filt.dtype)
    pattern = jnp.concatenate([lead_zero, flipped, trailing], axis=1)
    repeated = jnp.tile(pattern, (1, filter_len))
    return repeated[:, : filter_len * 2 * filter_len].reshape(count, filter_len, 2 * filter_len)


def make_windows(blocks, before):
    earlier = jnp.concatenate([before[:, :, None, :], blocks[:, :, :-1, :]], axis=2)
    return jnp.concatenate([earlier, blocks], axis=3)


def forward_conv(signal, before, toeplitz_mat):
    groups_here, group_size, seq_len = signal.shape
    filter_len = toeplitz_mat.shape[1]
    blocks = signal.reshape(groups_here, group_size, seq_len // filter_len, filter_len)
    window_rows = make_windows(blocks, before)
    result = contract("gam,gsnm->gsna", toeplitz_mat, window_rows)
    return (result.reshape(groups_here, group_size, seq_len), window_rows)


def backward_conv(grad_rows, after, toeplitz_mat):
    groups_here, group_size, seq_len = grad_rows.shape
    filter_len = toeplitz_mat.shape[1]
    blocks = grad_rows.reshape(groups_here, group_size, seq_len // filter_len, filter_len)
    spread = contract("gam,gsna->gsnm", toeplitz_mat, blocks)
    tail_part = contract("gam,gsa->gsm", toeplitz_mat, after)
    next_part = jnp.concatenate(
        [spread[:, :, 1:, :filter_len], tail_part[:, :, None, :filter_len]], axis=2
    )
    return (spread[:, :, :, filter_len:] + next_part).reshape(groups_here, group_size, seq_len)


def filter_grad(grad_rows, window_rows, filter_len):
    groups_here, group_size, seq_len = grad_rows.shape
    blocks = grad_rows.reshape(groups_here, group_size, seq_len // filter_len, filter_len)
    correlate = contract("gsna,gsnm->gam", blocks, window_rows)
    flattened = correlate.reshape(groups_here, filter_len * 2 * filter_len)
    flattened = jnp.concatenate(
        [flattened, jnp.zeros((groups_here, filter_len), jnp.float32)], axis=1
    )
    flattened = flattened.reshape(groups_here, filter_len, 2 * filter_len + 1)
    diagonals = jnp.sum(flattened, axis=1)
    return diagonals[:, 1 : filter_len + 1][:, ::-1]


def shards(queries, key_feats, value_feats, filters, grad_out):
    tokens, channels = queries.shape
    slab_groups, filter_len = filters.shape
    product = (
        (key_feats.astype(jnp.float32) * value_feats.astype(jnp.float32)).astype(jnp.bfloat16).T
    )
    grad_mix = (grad_out.astype(jnp.float32) * queries.astype(jnp.float32)).astype(jnp.bfloat16).T
    owners = lax.axis_size("ctx")
    own_width = channels // owners
    own_groups = own_width // G
    signal = lax.all_to_all(product, "ctx", split_axis=0, concat_axis=1, tiled=True)
    grad_rows = lax.all_to_all(grad_mix, "ctx", split_axis=0, concat_axis=1, tiled=True)
    seq_len = signal.shape[1]
    signal = signal.reshape(own_groups, G, seq_len)
    grad_rows = grad_rows.reshape(own_groups, G, seq_len)
    first_group = lax.axis_index("ctx") * own_groups
    own_filters = lax.dynamic_slice_in_dim(filters, first_group, own_groups, 0)
    toeplitz_mat = toeplitz(own_filters)
    zero_rim = jnp.zeros((own_groups, G, filter_len), jnp.bfloat16)
    conv_out, window_rows = forward_conv(signal, zero_rim, toeplitz_mat)
    conv_out = conv_out.astype(jnp.bfloat16).reshape(own_width, seq_len)
    conv_grad = (
        backward_conv(grad_rows, zero_rim, toeplitz_mat)
        .astype(jnp.bfloat16)
        .reshape(own_width, seq_len)
    )
    partial_grad = filter_grad(grad_rows, window_rows, filter_len)
    conv_rows = lax.all_to_all(conv_out, "ctx", split_axis=1, concat_axis=0, tiled=True)
    grad_back = lax.all_to_all(conv_grad, "ctx", split_axis=1, concat_axis=0, tiled=True)
    raw_filters = lax.all_gather(partial_grad, "ctx", axis=0, tiled=True)
    conv_f = conv_rows.T.astype(jnp.float32)
    back_f = grad_back.T.astype(jnp.float32)
    mixer_out = (queries.astype(jnp.float32) * conv_f).astype(jnp.bfloat16)
    grad_queries = (grad_out.astype(jnp.float32) * conv_f).astype(jnp.bfloat16)
    grad_keys = (back_f * value_feats.astype(jnp.float32)).astype(jnp.bfloat16)
    grad_values = (back_f * key_feats.astype(jnp.float32)).astype(jnp.bfloat16)
    square_sum = lax.psum(jnp.sum(raw_filters * raw_filters), "mp")
    grad_rms = jnp.sqrt(square_sum / (D // G * filter_len) + 1e-06)
    grad_filters = raw_filters * jnp.minimum(1.0, 1.0 / grad_rms)
    return (mixer_out, grad_queries, grad_keys, grad_values, grad_filters)


def solution(mesh):
    placed = (P("ctx", "mp"), P("ctx", "mp"), P("ctx", "mp"), P("mp", None), P("ctx", "mp"))
    return jax.shard_map(
        shards,
        mesh=mesh,
        in_specs=placed,
        out_specs=(P("ctx", "mp"), P("ctx", "mp"), P("ctx", "mp"), P("ctx", "mp"), P("mp", None)),
        check_vma=False,
    )
```

profile of v0, /device:TPU:1, one launch (start us, length us, event | category | flops | bytes accessed | tf_op | source)
XLA Modules:
  0.0 278.9 jit_solution(11719873778474944530)
XLA Ops:
  0.6 0.0 copy-start
  0.6 1.2 copy.28
  1.9 1.2 copy.33
  3.1 0.9 fusion.6
  4.1 12.9 %all-to-all-start.2 = ((bf16[64,16,256]{2,1,0:T(8,128)(2,1)}), bf16[64,16,256]{2,1,0:T(8,128)(2,1)S(1)}, u32[]{:S(2)}, u32[]{:S(2)}) async-start(bf16[64,16,256]{2,1,0:T(8,128)(2,1)} %bitcast.10), calls=%async_computation.2 | async-start | bytes 1048576 | tf_op jit(solution)/shard_map/all_to_all | solution.py:74
  17.0 0.0 copy-done
  17.0 0.1 rev.6
  17.1 0.1 pad.6.clone
  17.2 0.1 fusion.13
  17.3 0.4 tile.13
  17.7 0.4 slice_reduce_fusion
  18.2 0.1 convolution_bitcast_fusion.2
  18.3 14.5 %all-to-all-done.2 = bf16[64,16,256]{2,1,0:T(8,128)(2,1)S(1)} async-done(((bf16[64,16,256]{2,1,0:T(8,128)(2,1)}), bf16[64,16,256]{2,1,0:T(8,128)(2,1)S(1)}, u32[]{:S(2)}, u32[]{:S(2)}) %all-to-all-start.2) | async-done | bytes 524320 | tf_op jit(solution)/shard_map/all_to_all | solution.py:74
  32.8 0.2 copy.34
  32.9 0.2 reshape.85
  33.1 0.4 convolution_bitcast_fusion
  33.5 0.1 slice.27
  33.6 0.1 fusion.9
  33.8 0.0 copy-start.1
  33.8 0.2 convert_element_type.93
  34.0 1.1 copy.35
  35.0 0.0 copy-start.2
  35.0 7.2 %all-to-all-start.3 = ((bf16[16,64,256]{2,0,1:T(8,128)(2,1)}), bf16[16,64,256]{2,0,1:T(8,128)(2,1)S(1)}, u32[]{:S(2)}, u32[]{:S(2)}) async-start(bf16[16,64,256]{2,0,1:T(8,128)(2,1)} %copy.35), calls=%async_computation.3 | async-start | bytes 1048576 | tf_op jit(solution)/shard_map/all_to_all | solution.py:91
  42.2 0.0 copy-done.1
  42.2 1.0 copy.29
  43.2 0.0 copy-done.2
  43.2 1.0 copy.30
  44.2 12.8 %all-to-all-done.3 = bf16[16,64,256]{2,0,1:T(8,128)(2,1)S(1)} async-done(((bf16[16,64,256]{2,0,1:T(8,128)(2,1)}), bf16[16,64,256]{2,0,1:T(8,128)(2,1)S(1)}, u32[]{:S(2)}, u32[]{:S(2)}) %all-to-all-start.3) | async-done | bytes 524320 | tf_op jit(solution)/shard_map/all_to_all | solution.py:91
  57.0 1.5 fusion.2
  58.5 21.8 %all_to_all.52 = bf16[64,16,256]{2,1,0:T(8,128)(2,1)S(1)} all-to-all(bf16[64,16,256]{2,1,0:T(8,128)(2,1)S(1)} %bitcast.50), channel_id=1, replica_groups=mesh['ctx'=64,'mp'=8] {'ctx'}, dimensions={0} | all-to-all | bytes 1048576 | tf_op jit(solution)/shard_map/all_to_all | solution.py:73
  80.4 0.2 copy.31
  80.5 1.0 reshape_reshape.2
  81.5 2.4 convolution_convert_fusion
  83.9 1.2 convert_element_type.83
  85.1 1.1 copy.32
  86.2 8.1 %all-to-all-start.1 = ((bf16[16,64,256]{2,0,1:T(8,128)(2,1)}), bf16[16,64,256]{2,0,1:T(8,128)(2,1)S(1)}, u32[]{:S(2)}, u32[]{:S(2)}) async-start(bf16[16,64,256]{2,0,1:T(8,128)(2,1)} %copy.32), calls=%async_computation.1 | async-start | bytes 1048576 | tf_op jit(solution)/shard_map/all_to_all | solution.py:90
  94.4 1.0 copy.39
  95.4 1.5 convolution_bitcast_fusion.1
  96.9 0.1 copy.42
  97.1 0.3 pad_reduce_fusion
  97.4 0.3 reshape.87
  97.8 0.1 slice.29
  97.8 0.1 rev.7
  97.9 127.5 %all-gather = f32[64,1,128]{2,1,0:T(1,128)S(1)} all-gather(f32[1,1,128]{2,1,0:T(1,128)S(1)} %bitcast.57), channel_id=1, replica_groups=mesh['ctx'=64,'mp'=8] {'ctx'}, dimensions={0}, use_global_device_ids=true | all-gather | bytes 33280 | tf_op jit(solution)/shard_map/all_gather | solution.py:92
  225.5 0.7 multiply_reduce_fusion
  226.1 1.0 copy.40
  227.1 48.2 %psum.7 = f32[]{:T(128)} all-reduce(f32[]{:T(128)} %multiply_reduce_fusion), channel_id=1, replica_groups=mesh['ctx'=64,'mp'=8] {'mp'}, use_global_device_ids=true, to_apply=%region_2.0 | all-reduce | flops 1 | bytes 8 | tf_op jit(solution)/shard_map/psum | solution.py:99
  276.0 0.6 broadcast_multiply_fusion
  276.6 0.0 all-to-all-done.1
  276.6 0.2 fusion.5
  276.9 1.0 copy.37
  277.9 1.0 copy.38
  (8 shorter events, 0.1 us)
Async XLA Ops:
  0.6 16.4 %copy-start = (bf16[64,128]{1,0:T(8,128)(2,1)S(1)}, bf16[64,128]{1,0:T(8,128)(2,1)}, u32[]{:S(2)}) copy-start(bf16[64,128]{1,0:T(8,128)(2,1)} %param.8) | copy-start | bytes 49156
  4.1 28.7 %all-to-all-start.2 = ((bf16[64,16,256]{2,1,0:T(8,128)(2,1)}), bf16[64,16,256]{2,1,0:T(8,128)(2,1)S(1)}, u32[]{:S(2)}, u32[]{:S(2)}) async-start(bf16[64,16,256]{2,1,0:T(8,128)(2,1)} %bitcast.10), calls=%async_computation.2 | async-start | bytes 1048576 | tf_op jit(solution)/shard_map/all_to_all | solution.py:74
  33.8 8.5 %copy-start.1 = (bf16[256,1024]{1,0:T(8,128)(2,1)S(1)}, bf16[256,1024]{1,0:T(8,128)(2,1)}, u32[]{:S(2)}) copy-start(bf16[256,1024]{1,0:T(8,128)(2,1)} %param.6) | copy-start | bytes 1572868
  35.0 8.2 %copy-start.2 = (bf16[256,1024]{1,0:T(8,128)(2,1)S(1)}, bf16[256,1024]{1,0:T(8,128)(2,1)}, u32[]{:S(2)}) copy-start(bf16[256,1024]{1,0:T(8,128)(2,1)} %param.7) | copy-start | bytes 1572868
  35.0 22.0 %all-to-all-start.3 = ((bf16[16,64,256]{2,0,1:T(8,128)(2,1)}), bf16[16,64,256]{2,0,1:T(8,128)(2,1)S(1)}, u32[]{:S(2)}, u32[]{:S(2)}) async-start(bf16[16,64,256]{2,0,1:T(8,128)(2,1)} %copy.35), calls=%async_computation.3 | async-start | bytes 1048576 | tf_op jit(solution)/shard_map/all_to_all | solution.py:91
  86.2 190.4 %all-to-all-start.1 = ((bf16[16,64,256]{2,0,1:T(8,128)(2,1)}), bf16[16,64,256]{2,0,1:T(8,128)(2,1)S(1)}, u32[]{:S(2)}, u32[]{:S(2)}) async-start(bf16[16,64,256]{2,0,1:T(8,128)(2,1)} %copy.32), calls=%async_computation.1 | async-start | bytes 1048576 | tf_op jit(solution)/shard_map/all_to_all | solution.py:90
where the time goes:
time: 279 us
  blocking collectives  198 us (71%)
  starting transfers between devices  28.2 us (10%)
  waiting for transfers between devices  27.3 us (10%)
  local copies, waits for them, and re-layouts  15.6 us (6%)
  matrix products  4.52 us (2%)
  other arithmetic  4.21 us (2%)
    all_gather x1, blocking collectives, shards(): raw_filters = lax.all_gather(partial_grad, 'ctx', axis=0, tiled=True)  128 us
    psum x1, blocking collectives, shards(): square_sum = lax.psum(jnp.sum(raw_filters * raw_filters), 'mp')  48.2 us
    all_to_all x1, blocking collectives, shards(): lax.all_to_all(product, 'ctx', split_axis=0, concat_axis=1, tiled=True)  21.8 us
    all_to_all x1, waiting for transfers between devices, shards(): lax.all_to_all(grad_mix, 'ctx', split_axis=0, concat_axis=1, tiled=True)  14.5 us
    all_to_all x1, starting transfers between devices, shards(): lax.all_to_all(grad_mix, 'ctx', split_axis=0, concat_axis=1, tiled=True)  12.9 us
    all_to_all x1, waiting for transfers between devices, shards(): lax.all_to_all(conv_grad, 'ctx', split_axis=1, concat_axis=0, tiled=True)  12.8 us
    unnamed x15, local copies, waits for them, and re-layouts  8.66 us
    all_to_all x1, starting transfers between devices, shards(): lax.all_to_all(conv_out, 'ctx', split_axis=1, concat_axis=0, tiled=True)  8.11 us
  transfers between devices with their start and end apart: 3, of which 2 were waited for; matrix products, arithmetic and copies ran while one was open for 3% of the time, Pallas kernels for 0%

commit v1 on v0

v1 whole, which is shorter than its diff:
```python
import jax
import jax.numpy as jnp
from jax import lax
from jax.experimental import pallas as pl
from jax.experimental.pallas import tpu as pltpu
from jax.sharding import Mesh, PartitionSpec as P

D = 8192
G = 16
K = 128
B = 64
W = 2 * K
LANES = 128
TILE_GROUPS = LANES // G
CTX = ("y", "zl", "x")
MP = ("zh", "core")


def gate(first_ref, second_ref):
    first = first_ref[...].astype(jnp.float32)
    return (first * second_ref[...].astype(jnp.float32)).astype(jnp.bfloat16)


def windows(rows, blocks):
    return jnp.concatenate([rows[n * B : n * B + W] for n in range(blocks)], axis=1)


def group_of_lane(shape):
    return (lax.broadcasted_iota(jnp.int32, shape, 1) % LANES) // G


def filter_kernel(q_ref, k_ref, v_ref, go_ref, after_ref, raw_ref):
    product = gate(k_ref, v_ref)
    mix = gate(go_ref, q_ref)
    blocks = product.shape[0] // B
    rows = jnp.concatenate([mix, after_ref[...], jnp.zeros((W - K - B, LANES), jnp.bfloat16)], axis=0)
    wins = windows(rows, blocks)
    left = jnp.concatenate([product[n * B : (n + 1) * B] for n in range(blocks)], axis=1)
    group = group_of_lane(left.shape)
    zero = jnp.zeros_like(left)
    left = jnp.concatenate([jnp.where(group == g, left, zero) for g in range(TILE_GROUPS)], axis=0)
    pairs = lax.dot_general(left, wins, (((1,), (1,)), ((), ())), preferred_element_type=jnp.float32)
    sub = lax.broadcasted_iota(jnp.int32, (8, W), 0)
    for g in range(TILE_GROUPS):
        total = pairs[g * B : g * B + 8]
        for r in range(1, B // 8):
            total = total + pltpu.roll(pairs[g * B + 8 * r : g * B + 8 * r + 8], W - 8 * r, 1)
        for bit in (1, 2, 4):
            total = jnp.where((sub & bit) != 0, pltpu.roll(total, W - bit, 1), total)
        raw_ref[g : g + 1, :] = jnp.sum(total[:, :K], axis=0, keepdims=True)


def toeplitz_rows(rows_ref):
    mats = []
    for g in range(TILE_GROUPS):
        row = jnp.broadcast_to(rows_ref[g : g + 1, :], (B, W))
        mats.append(pltpu.roll(row, 0, 1, stride=1, stride_axis=0).astype(jnp.bfloat16))
    return jnp.concatenate(mats, axis=0)


def convolve(rows_ref, rows, blocks):
    full = jnp.dot(toeplitz_rows(rows_ref), windows(rows, blocks), preferred_element_type=jnp.float32)
    group = group_of_lane((B, blocks * LANES))
    total = full[:B]
    for g in range(1, TILE_GROUPS):
        total = jnp.where(group == g, full[g * B : (g + 1) * B], total)
    total = total.astype(jnp.bfloat16).astype(jnp.float32)
    return jnp.concatenate([total[:, n * LANES : (n + 1) * LANES] for n in range(blocks)], axis=0)


def conv_kernel(
    q_ref, k_ref, v_ref, go_ref, before_ref, after_ref, forward_ref, backward_ref, mo_ref, gq_ref, gk_ref, gv_ref
):
    product = gate(k_ref, v_ref)
    mix = gate(go_ref, q_ref)
    blocks = product.shape[0] // B
    pad = jnp.zeros((W - K - B, LANES), jnp.bfloat16)
    out = convolve(forward_ref, jnp.concatenate([before_ref[...], product, pad], axis=0), blocks)
    mo_ref[...] = (q_ref[...].astype(jnp.float32) * out).astype(jnp.bfloat16)
    gq_ref[...] = (go_ref[...].astype(jnp.float32) * out).astype(jnp.bfloat16)
    back = convolve(backward_ref, jnp.concatenate([mix, after_ref[...], pad], axis=0), blocks)
    gk_ref[...] = (back * v_ref[...].astype(jnp.float32)).astype(jnp.bfloat16)
    gv_ref[...] = (back * k_ref[...].astype(jnp.float32)).astype(jnp.bfloat16)


def product_of(first, second):
    return (first.astype(jnp.float32) * second.astype(jnp.float32)).astype(jnp.bfloat16)


def sum_over(value, axes):
    size = lax.axis_size(axes)
    spread = jnp.broadcast_to(value[None], (size,) + value.shape)
    return jnp.sum(lax.all_to_all(spread, axes, split_axis=0, concat_axis=0, tiled=True), axis=0)


def shards(queries, key_feats, value_feats, filters, grad_out):
    tokens, channels = queries.shape
    slab_groups = filters.shape[0]
    owners = lax.axis_size(CTX)
    tail = product_of(key_feats[tokens - K :], value_feats[tokens - K :])
    head = product_of(grad_out[:K], queries[:K])
    after = lax.ppermute(head, CTX, [(i + 1, i) for i in range(owners - 1)])
    before = lax.ppermute(tail, CTX, [(i, i + 1) for i in range(owners - 1)])

    tiles = channels // LANES
    whole = pl.BlockSpec((tokens, LANES), lambda i: (0, i))
    halo = pl.BlockSpec((K, LANES), lambda i: (0, i))
    group_rows = pl.BlockSpec((TILE_GROUPS, W), lambda i: (i, 0))
    raw = pl.pallas_call(
        filter_kernel,
        grid=(tiles,),
        in_specs=[whole] * 4 + [halo],
        out_specs=pl.BlockSpec((TILE_GROUPS, K), lambda i: (i, 0)),
        out_shape=jax.ShapeDtypeStruct((slab_groups, K), jnp.float32),
        cost_estimate=pl.CostEstimate(flops=10**9, bytes_accessed=5 * 2**19, transcendentals=0),
        name="filter_grad",
    )(queries, key_feats, value_feats, grad_out, after)

    filt = filters.astype(jnp.float32)
    zeros = jnp.zeros((slab_groups, W - K), jnp.float32)
    backward_rows = jnp.concatenate([filt, zeros], axis=1)
    forward_rows = jnp.concatenate([zeros[:, :1], filt[:, ::-1], zeros[:, 1:]], axis=1)
    wide = jax.ShapeDtypeStruct((tokens, channels), jnp.bfloat16)
    mixer_out, grad_queries, grad_keys, grad_values = pl.pallas_call(
        conv_kernel,
        grid=(tiles,),
        in_specs=[whole] * 4 + [halo] * 2 + [group_rows] * 2,
        out_specs=[whole] * 4,
        out_shape=[wide] * 4,
        cost_estimate=pl.CostEstimate(flops=2 * 10**9, bytes_accessed=9 * 2**19, transcendentals=0),
        name="conv",
    )(queries, key_feats, value_feats, grad_out, before, after, forward_rows, backward_rows)

    raw = sum_over(raw, ("zl", "x"))
    raw = sum_over(raw, ("y",))
    squares = sum_over(jnp.sum(raw * raw, axis=0, keepdims=True), MP)
    grad_rms = jnp.sqrt(jnp.sum(squares) / (D // G * K) + 1e-06)
    grad_filters = raw * jnp.minimum(1.0, 1.0 / grad_rms)
    return (mixer_out, grad_queries, grad_keys, grad_values, grad_filters)


def solution(mesh):
    fine = Mesh(mesh.devices.reshape(8, 2, 4, 4, 2), CTX + MP)
    placed = (P(CTX, MP), P(CTX, MP), P(CTX, MP), P(MP, None), P(CTX, MP))
    return jax.shard_map(
        shards,
        mesh=fine,
        in_specs=placed,
        out_specs=(P(CTX, MP), P(CTX, MP), P(CTX, MP), P(CTX, MP), P(MP, None)),
        check_vma=False,
    )
```

time: 279 us -> 77.8 us (0.28)
  blocking collectives: 198 us -> 16.6 us
  Pallas kernels: 0 us -> 15 us
  waiting for transfers between devices: 27.3 us -> 12.3 us
  local copies, waits for them, and re-layouts: 15.6 us -> 4.29 us
  matrix products: 4.52 us -> 0 us
  starting transfers between devices: 28.2 us -> 23.7 us
    all_gather x1 -> x0, blocking collectives: 128 us -> none  [shards(): raw_filters = lax.all_gather(partial_grad, 'ctx', axis=0, tiled=True)]
    psum x1 -> x0, blocking collectives: 48.2 us -> none  [shards(): square_sum = lax.psum(jnp.sum(raw_filters * raw_filters), 'mp')]
    all_to_all x3 -> x2, waiting for transfers between devices: 27.3 us -> 5.94 us  [sum_over(): lax.all_to_all(spread, axes, split_axis=0, concat_axis=0, tiled=True)]
    pallas_call x0 -> x2, Pallas kernels: none -> 15 us  [the longest x1 7.59 us: shards(): pl.pallas_call(filter_kernel, grid=(tiles,), in_specs=[whole] * 4 + [halo...]
    all_to_all x3 -> x2, starting transfers between devices: 28.2 us -> 20.5 us  [sum_over(): lax.all_to_all(spread, axes, split_axis=0, concat_axis=0, tiled=True)]
    unnamed x15 -> x10, local copies, waits for them, and re-layouts: 8.66 us -> 1.4 us
    ppermute x0 -> x2, waiting for transfers between devices: none -> 6.41 us  [the longest x1 6.4 us: shards(): after = lax.ppermute(head, CTX, [(i + 1, i) for i in range(owners - 1)])]
    all_to_all x1, blocking collectives: 21.8 us -> 16.6 us  [sum_over(): lax.all_to_all(spread, axes, split_axis=0, concat_axis=0, tiled=True)]
  transfers between devices with their start and end apart: 3 -> 4, of which waited for: 2 -> 2; matrix products, arithmetic and copies ran while one was open for 3% -> 3% of each run, Pallas kernels for 0% -> 10%
where the time goes in v1:
time: 77.8 us; the launch traced here: 76.6 us
  starting transfers between devices  23.7 us (30%)
  blocking collectives  16.6 us (21%)
  Pallas kernels  15 us (19%)
  waiting for transfers between devices  12.3 us (16%)
  local copies, waits for them, and re-layouts  4.29 us (6%)
  other arithmetic  3.17 us (4%)
  between operations  1.41 us (2%)
    all_to_all x2, starting transfers between devices, sum_over(): lax.all_to_all(spread, axes, split_axis=0, concat_axis=0, tiled=True)  20.5 us
    all_to_all x1, blocking collectives, sum_over(): lax.all_to_all(spread, axes, split_axis=0, concat_axis=0, tiled=True)  16.6 us
    pallas_call x1, Pallas kernels, shards(): pl.pallas_call(filter_kernel, grid=(tiles,), in_specs=[whole] * 4 + [halo...  7.59 us
    pallas_call x1, Pallas kernels, shards(): pl.pallas_call(conv_kernel, grid=(tiles,), in_specs=[whole] * 4 + [halo]...  7.44 us
    ppermute x1, waiting for transfers between devices, shards(): after = lax.ppermute(head, CTX, [(i + 1, i) for i in range(owners - 1)])  6.4 us
    all_to_all x2, waiting for transfers between devices, sum_over(): lax.all_to_all(spread, axes, split_axis=0, concat_axis=0, tiled=True)  5.94 us
    broadcast_in_dim x3, local copies, waits for them, and re-layouts, sum_over(): spread = jnp.broadcast_to(value[None], (size,) + value.shape)  2.09 us
    ppermute x1, starting transfers between devices, shards(): before = lax.ppermute(tail, CTX, [(i, i + 1) for i in range(owners - 1)])  1.85 us
  transfers between devices with their start and end apart: 4, of which 2 were waited for; matrix products, arithmetic and copies ran while one was open for 3% of the time, Pallas kernels for 10%

profile of v1, /device:TPU:1, one launch (start us, length us, event | category | flops | bytes accessed | tf_op | source)
XLA Modules:
  0.0 76.6 jit_solution(12143012882482584205)
XLA Ops:
  0.6 1.1 %multiply_convert_fusion = bf16[128,1024]{1,0:T(8,128)(2,1)S(1)} fusion(bf16[256,1024]{1,0:T(8,128)(2,1)} %q_ref.3, bf16[256,1024]{1,0:T(8,128)(2,1)} %go_ref.3), kind=kLoop, calls=%fused_computation | loop fusion | flops 524288 | bytes 786432 | tf_op jit(solution)/shard_map/convert_element_type | solution.py:87
  1.7 1.3 %collective-permute-start.1 = (bf16[128,1024]{1,0:T(8,128)(2,1)S(1)}, bf16[128,1024]{1,0:T(8,128)(2,1)S(1)}, u32[]{:S(2)}, u32[]{:S(2)}) collective-permute-start(bf16[128,1024]{1,0:T(8,128)(2,1)S(1)} %multiply_convert_fusion), channel_id=1, source_target_pairs={{8,0},{16,8},{24,16},{32,24},{40,32},{48,40},{56,48},{64,56},{72,6... | collective-permute-start | bytes 786440 | tf_op jit(solution)/shard_map/ppermute | solution.py:102
  3.0 6.4 %collective-permute-done.1.after_ref = bf16[128,1024]{1,0:T(8,128)(2,1)S(1)} collective-permute-done((bf16[128,1024]{1,0:T(8,128)(2,1)S(1)}, bf16[128,1024]{1,0:T(8,128)(2,1)S(1)}, u32[]{:S(2)}, u32[]{:S(2)}) %collective-permute-start.1) | collective-permute-done | bytes 262176 | tf_op jit(solution)/shard_map/ppermute | solution.py:102
  9.4 0.0 copy-start.3
  9.4 0.7 copy-done.3
  10.1 7.6 %filter_grad.1 = f32[64,128]{1,0:T(8,128)} custom-call(bf16[256,1024]{1,0:T(8,128)(2,1)} %q_ref.3, bf16[256,1024]{1,0:T(8,128)(2,1)} %k_ref.3, bf16[256,1024]{1,0:T(8,128)(2,1)} %v_ref.3, bf16[256,1024]{1,0:T(8,128)(2,1)} %go_ref.3, bf16[128,1024]{1,0:T(8,128)(2,1)} %copy-done.3), custom_call_target="tpu_custom_call" | custom-call | flops 1000000000 | bytes 2621440 | tf_op jit(solution)/shard_map/filter_grad/pallas_call | solution.py:109
  17.7 0.8 %broadcast_in_dim.6 = f32[8,64,128]{2,1,0:T(8,128)S(1)} broadcast(f32[64,128]{1,0:T(8,128)} %filter_grad.1), dimensions={1,2} | broadcast | bytes 294912 | tf_op jit(solution)/shard_map/broadcast_in_dim | solution.py:92
  18.5 16.6 %all_to_all.15 = f32[8,64,128]{2,1,0:T(8,128)S(1)} all-to-all(f32[8,64,128]{2,1,0:T(8,128)S(1)} %broadcast_in_dim.6), channel_id=1, replica_groups=mesh['y'=8,'zl'=2,'x'=4,'zh'=4,'core'=2] {'zl','x'}, dimensions={0} | all-to-all | bytes 524288 | tf_op jit(solution)/shard_map/all_to_all | solution.py:93
  35.2 0.0 copy-start
  35.2 0.0 copy-start.1
  35.2 0.7 broadcast_in_dim.7
  35.9 6.8 %all-to-all-start.1 = ((f32[8,64,128]{2,1,0:T(8,128)}), f32[8,64,128]{2,1,0:T(8,128)S(1)}, u32[]{:S(2)}, u32[]{:S(2)}) async-start(f32[8,64,128]{2,1,0:T(8,128)} %broadcast_in_dim.7), calls=%async_computation.1 | async-start | bytes 524288 | tf_op jit(solution)/shard_map/all_to_all | solution.py:93
  42.7 0.0 copy-done
  42.7 0.0 copy-done.1
  42.7 0.0 copy-start.2
  42.7 0.1 multiply_convert_fusion.1
  42.8 1.9 %collective-permute-start = (bf16[128,1024]{1,0:T(8,128)(2,1)S(1)}, bf16[128,1024]{1,0:T(8,128)(2,1)S(1)}, u32[]{:S(2)}, u32[]{:S(2)}) collective-permute-start(bf16[128,1024]{1,0:T(8,128)(2,1)S(1)} %multiply_convert_fusion.1), channel_id=1, source_target_pairs={{0,8},{8,16},{16,24},{24,32},{32,40},{40,48},{48,56},{56,64},{64,7... | collective-permute-start | bytes 786440 | tf_op jit(solution)/shard_map/ppermute | solution.py:103
  44.7 0.0 copy-done.2
  44.7 0.1 rev.3
  44.8 0.6 concatenate.7.backward_ref
  45.4 0.1 pad.3.clone
  45.5 0.7 maximum_maximum_fusion.forward_ref
  46.2 5.9 %all-to-all-done.1 = f32[8,64,128]{2,1,0:T(8,128)S(1)} async-done(((f32[8,64,128]{2,1,0:T(8,128)}), f32[8,64,128]{2,1,0:T(8,128)S(1)}, u32[]{:S(2)}, u32[]{:S(2)}) %all-to-all-start.1) | async-done | bytes 262176 | tf_op jit(solution)/shard_map/all_to_all | solution.py:93
  52.2 0.6 broadcast_in_dim.8
  52.8 13.7 %all-to-all-start.2 = ((f32[8,1,128]{2,1,0:T(1,128)}), f32[8,1,128]{2,1,0:T(1,128)S(1)}, u32[]{:S(2)}, u32[]{:S(2)}) async-start(f32[8,1,128]{2,1,0:T(1,128)} %broadcast_in_dim.8), calls=%async_computation.2 | async-start | bytes 8192 | tf_op jit(solution)/shard_map/all_to_all | solution.py:93
  66.5 0.0 collective-permute-done.before_ref
  66.5 0.0 copy-start.4
  66.5 0.7 copy-done.4
  67.2 7.4 %conv.1 = (bf16[256,1024]{1,0:T(8,128)(2,1)}, bf16[256,1024]{1,0:T(8,128)(2,1)}, bf16[256,1024]{1,0:T(8,128)(2,1)}, bf16[256,1024]{1,0:T(8,128)(2,1)}) custom-call(bf16[256,1024]{1,0:T(8,128)(2,1)} %q_ref.3, bf16[256,1024]{1,0:T(8,128)(2,1)} %k_ref.3, bf16[256,1024]{1,0:T(8,128)(2,1)} %v_ref.3, bf16[256,1024]{1,0:T(8,128)(2,1)} %go_ref.3, ...), custom_call_target="tpu_custom_call" | custom-call | flops 2000000000 | bytes 4718592 | tf_op jit(solution)/shard_map/conv/pallas_call | solution.py:124
  74.6 0.0 all-to-all-done.2
  74.6 0.6 reduce_sum.43
  75.9 0.6 broadcast_multiply_fusion
  (5 shorter events, 0.1 us)
Async XLA Ops:
  1.7 7.7 %collective-permute-start.1 = (bf16[128,1024]{1,0:T(8,128)(2,1)S(1)}, bf16[128,1024]{1,0:T(8,128)(2,1)S(1)}, u32[]{:S(2)}, u32[]{:S(2)}) collective-permute-start(bf16[128,1024]{1,0:T(8,128)(2,1)S(1)} %multiply_convert_fusion), channel_id=1, source_target_pairs={{8,0},{16,8},{24,16},{32,24},{40,32},{48,40},{56,48},{64,56},{72,6... | collective-permute-start | bytes 786440 | tf_op jit(solution)/shard_map/ppermute | solution.py:102
  9.4 0.7 copy-start.3
  35.2 7.6 %copy-start = (bf16[256,1024]{1,0:T(8,128)(2,1)S(1)}, bf16[256,1024]{1,0:T(8,128)(2,1)}, u32[]{:S(2)}) copy-start(bf16[256,1024]{1,0:T(8,128)(2,1)} %k_ref.3) | copy-start | bytes 1572868
  35.2 7.6 %copy-start.1 = (bf16[256,1024]{1,0:T(8,128)(2,1)S(1)}, bf16[256,1024]{1,0:T(8,128)(2,1)}, u32[]{:S(2)}) copy-start(bf16[256,1024]{1,0:T(8,128)(2,1)} %v_ref.3) | copy-start | bytes 1572868
  35.9 16.3 %all-to-all-start.1 = ((f32[8,64,128]{2,1,0:T(8,128)}), f32[8,64,128]{2,1,0:T(8,128)S(1)}, u32[]{:S(2)}, u32[]{:S(2)}) async-start(f32[8,64,128]{2,1,0:T(8,128)} %broadcast_in_dim.7), calls=%async_computation.1 | async-start | bytes 524288 | tf_op jit(solution)/shard_map/all_to_all | solution.py:93
  42.7 2.0 %copy-start.2 = (bf16[64,128]{1,0:T(8,128)(2,1)S(1)}, bf16[64,128]{1,0:T(8,128)(2,1)}, u32[]{:S(2)}) copy-start(bf16[64,128]{1,0:T(8,128)(2,1)} %param.8) | copy-start | bytes 49156
  42.8 23.7 %collective-permute-start = (bf16[128,1024]{1,0:T(8,128)(2,1)S(1)}, bf16[128,1024]{1,0:T(8,128)(2,1)S(1)}, u32[]{:S(2)}, u32[]{:S(2)}) collective-permute-start(bf16[128,1024]{1,0:T(8,128)(2,1)S(1)} %multiply_convert_fusion.1), channel_id=1, source_target_pairs={{0,8},{8,16},{16,24},{24,32},{32,40},{40,48},{48,56},{56,64},{64,7... | collective-permute-start | bytes 786440 | tf_op jit(solution)/shard_map/ppermute | solution.py:103
  52.8 21.8 %all-to-all-start.2 = ((f32[8,1,128]{2,1,0:T(1,128)}), f32[8,1,128]{2,1,0:T(1,128)S(1)}, u32[]{:S(2)}, u32[]{:S(2)}) async-start(f32[8,1,128]{2,1,0:T(1,128)} %broadcast_in_dim.8), calls=%async_computation.2 | async-start | bytes 8192 | tf_op jit(solution)/shard_map/all_to_all | solution.py:93
  66.5 0.7 copy-start.4

commit v2 on v1

v2 whole, which is shorter than its diff:
```python
import functools

import jax
import jax.numpy as jnp
from jax import lax
from jax.experimental import pallas as pl
from jax.experimental.pallas import tpu as pltpu
from jax.sharding import Mesh, PartitionSpec as P

D = 8192
G = 16
K = 128
B = 32
FB = 32
W = 2 * K
LANES = 128
UNROLL = 4
TILE_GROUPS = LANES // G
CTX = ("y", "zl", "x")
MP = ("zh", "core")
HBM = pl.BlockSpec(memory_space=pl.ANY)
VMEM = pl.BlockSpec(memory_space=pltpu.VMEM)


def product_of(first, second):
    return (first.astype(jnp.float32) * second.astype(jnp.float32)).astype(jnp.bfloat16)


def blocks_of(rows, size):
    return jnp.concatenate([rows[n : n + size] for n in range(0, rows.shape[0], size)], axis=1)


def windows(rows, size):
    return jnp.concatenate([rows[n : n + W] for n in range(0, rows.shape[0] - W + size, size)], axis=1)


def group_of_lane(shape):
    return (lax.broadcasted_iota(jnp.int32, shape, 1) % LANES) // G


def correlate(product, following, tile, rows_ref):
    left = blocks_of(product, FB)
    group = group_of_lane(left.shape)
    zero = jnp.zeros_like(left)
    left = jnp.concatenate([jnp.where(group == g, left, zero) for g in range(TILE_GROUPS)], axis=0)
    pad = jnp.zeros((product.shape[0] - FB + W - following.shape[0], LANES), jnp.bfloat16)
    wins = windows(jnp.concatenate([following, pad], axis=0), FB)
    pairs = lax.dot_general(left, wins, (((1,), (1,)), ((), ())), preferred_element_type=jnp.float32)
    for g in range(TILE_GROUPS):
        total = pairs[g * FB : g * FB + 8]
        for r in range(8, FB, 8):
            total = total + pltpu.roll(pairs[g * FB + r : g * FB + r + 8], W - r, 1)
        rows_ref[pl.ds((tile * TILE_GROUPS + g) * 8, 8), :] = total


def fold(rows_ref):
    rows = rows_ref[...]
    sub = lax.broadcasted_iota(jnp.int32, rows.shape, 0)
    for bit in (1, 2, 4):
        rows = jnp.where((sub & bit) != 0, pltpu.roll(rows, W - bit, 1), rows)
    return jnp.sum(rows[:, :K].reshape(rows.shape[0] // 8, 8, K), axis=1)


def lanes_of(tile):
    return pl.ds(pl.multiple_of(tile * LANES, LANES), LANES)


def copies_of(pairs, tile, sems):
    c = lanes_of(tile)
    return [pltpu.make_async_copy(src.at[:, c], dst.at[:, c], sems.at[n, tile]) for n, (src, dst) in enumerate(pairs)]


def start_all(pairs, tiles, sems):
    @pl.loop(0, tiles)
    def _(t):
        for copy in copies_of(pairs, t, sems):
            copy.start()


def local_kernel(q_hbm, k_hbm, v_hbm, go_hbm, raw_ref, q_buf, k_buf, v_buf, go_buf, rows, sems):
    pairs = ((k_hbm, k_buf), (v_hbm, v_buf), (go_hbm, go_buf), (q_hbm, q_buf))
    tiles = q_buf.shape[1] // LANES
    start_all(pairs, tiles, sems)

    @pl.loop(0, tiles, unroll=2)
    def _(t):
        c = lanes_of(t)
        for copy in copies_of(pairs, t, sems):
            copy.wait()
        correlate(product_of(k_buf[:, c], v_buf[:, c]), product_of(go_buf[:, c], q_buf[:, c]), t, rows)

    raw_ref[...] = fold(rows)


def edge_kernel(tail_ref, after_ref, local_ref, raw_ref, rows):
    @pl.loop(0, tail_ref.shape[1] // LANES, unroll=UNROLL)
    def _(t):
        c = lanes_of(t)
        following = jnp.concatenate([jnp.zeros((K, LANES), jnp.bfloat16), after_ref[:, c]], axis=0)
        correlate(tail_ref[:, c], following, t, rows)

    raw_ref[...] = local_ref[...] + fold(rows)


def toeplitz_rows(rows_ref, t):
    mats = []
    for g in range(TILE_GROUPS):
        row = jnp.broadcast_to(rows_ref[pl.ds(t * TILE_GROUPS + g, 1), :], (B, W))
        mats.append(pltpu.roll(row, 0, 1, stride=1, stride_axis=0).astype(jnp.bfloat16))
    return jnp.concatenate(mats, axis=0)


def convolve(mats, rows):
    blocks = (rows.shape[0] - K) // B
    pad = jnp.zeros((W - K - B, LANES), jnp.bfloat16)
    wins = windows(jnp.concatenate([rows, pad], axis=0), B)
    full = jnp.dot(mats, wins, preferred_element_type=jnp.float32)
    group = group_of_lane((B, blocks * LANES))
    total = full[:B]
    for g in range(1, TILE_GROUPS):
        total = jnp.where(group == g, full[g * B : (g + 1) * B], total)
    total = total.astype(jnp.bfloat16).astype(jnp.float32)
    return jnp.concatenate([total[:, n * LANES : (n + 1) * LANES] for n in range(blocks)], axis=0)


def conv_kernel(
    causal, a_hbm, b_hbm, x_hbm, y_hbm, halo_ref, filter_ref, ox_hbm, oy_hbm,
    a_buf, b_buf, x_buf, y_buf, ox_buf, oy_buf, in_sems, out_sems,
):
    tiles = a_buf.shape[1] // LANES
    ins = ((a_hbm, a_buf), (b_hbm, b_buf), (x_hbm, x_buf), (y_hbm, y_buf))
    outs = ((ox_buf, ox_hbm), (oy_buf, oy_hbm))
    start_all(ins, tiles, in_sems)

    @pl.loop(0, tiles, unroll=2)
    def _(t):
        c = lanes_of(t)
        mats = toeplitz_rows(filter_ref, t)
        for copy in copies_of(ins, t, in_sems):
            copy.wait()
        own, halo = product_of(a_buf[:, c], b_buf[:, c]), halo_ref[:, c]
        out = convolve(mats, jnp.concatenate([halo, own] if causal else [own, halo], axis=0))
        ox_buf[:, c] = (out * x_buf[:, c].astype(jnp.float32)).astype(jnp.bfloat16)
        oy_buf[:, c] = (out * y_buf[:, c].astype(jnp.float32)).astype(jnp.bfloat16)
        for copy in copies_of(outs, t, out_sems):
            copy.start()

    @pl.loop(0, tiles)
    def _(t):
        for copy in copies_of(outs, t, out_sems):
            copy.wait()


def local_filter(q, k, v, go, slab_groups):
    tokens, channels = q.shape
    return pl.pallas_call(
        local_kernel,
        in_specs=[HBM] * 4,
        out_specs=VMEM,
        out_shape=jax.ShapeDtypeStruct((slab_groups, K), jnp.float32),
        scratch_shapes=[pltpu.VMEM((tokens, channels), jnp.bfloat16)] * 4
        + [pltpu.VMEM((slab_groups * 8, W), jnp.float32), pltpu.SemaphoreType.DMA((4, channels // LANES))],
        cost_estimate=pl.CostEstimate(flops=3 * 10**9, bytes_accessed=2**21, transcendentals=0),
        compiler_params=pltpu.CompilerParams(vmem_limit_bytes=8 << 20),
        name="local_filter",
    )(q, k, v, go)


def edge_filter(tail, after, local):
    return pl.pallas_call(
        edge_kernel,
        in_specs=[VMEM] * 3,
        out_specs=VMEM,
        out_shape=jax.ShapeDtypeStruct(local.shape, jnp.float32),
        scratch_shapes=[pltpu.VMEM((local.shape[0] * 8, W), jnp.float32)],
        cost_estimate=pl.CostEstimate(flops=10**9, bytes_accessed=2**19, transcendentals=0),
        compiler_params=pltpu.CompilerParams(vmem_limit_bytes=4 << 20),
        name="edge_filter",
    )(tail, after, local)


def conv(causal, signal, factors, halo, filter_rows):
    wide = jax.ShapeDtypeStruct(signal[0].shape, jnp.bfloat16)
    buffer = pltpu.VMEM(wide.shape, jnp.bfloat16)
    sems = [pltpu.SemaphoreType.DMA((n, wide.shape[1] // LANES)) for n in (4, 2)]
    return pl.pallas_call(
        functools.partial(conv_kernel, causal),
        in_specs=[HBM] * 4 + [VMEM] * 2,
        out_specs=[HBM] * 2,
        out_shape=[wide] * 2,
        scratch_shapes=[buffer] * 6 + sems,
        cost_estimate=pl.CostEstimate(flops=2 * 10**9, bytes_accessed=3 * 2**20, transcendentals=0),
        compiler_params=pltpu.CompilerParams(vmem_limit_bytes=10 << 20),
        name="forward_conv" if causal else "backward_conv",
    )(*signal, *factors, halo, filter_rows)


def sum_over(value, axes):
    size = lax.axis_size(axes)
    spread = jnp.broadcast_to(value[None], (size,) + value.shape)
    return jnp.sum(lax.all_to_all(spread, axes, split_axis=0, concat_axis=0, tiled=True), axis=0)


def shards(queries, key_feats, value_feats, filters, grad_out):
    tokens = queries.shape[0]
    slab_groups = filters.shape[0]
    owners = lax.axis_size(CTX)
    head = product_of(grad_out[:K], queries[:K])
    after = lax.ppermute(head, CTX, [(i + 1, i) for i in range(owners - 1)])
    tail = product_of(key_feats[tokens - K :], value_feats[tokens - K :])
    before = lax.ppermute(tail, CTX, [(i, i + 1) for i in range(owners - 1)])

    local = local_filter(queries, key_feats, value_feats, grad_out, slab_groups)
    raw = edge_filter(tail, after, local)

    filt = filters.astype(jnp.float32)
    zeros = jnp.zeros((slab_groups, W - K), jnp.float32)
    backward_rows = jnp.concatenate([filt, zeros], axis=1)
    forward_rows = jnp.concatenate([zeros[:, :1], filt[:, ::-1], zeros[:, 1:]], axis=1)

    raw, before = lax.optimization_barrier((raw, before))
    forward = conv(True, (key_feats, value_feats), (queries, grad_out), before, forward_rows)
    raw = sum_over(raw, ("zl", "x"))
    raw, after, forward = lax.optimization_barrier((raw, after, forward))
    backward = conv(False, (grad_out, queries), (value_feats, key_feats), after, backward_rows)
    raw = sum_over(raw, ("y",))
    raw, backward = lax.optimization_barrier((raw, backward))
    squares = sum_over(jnp.sum(raw * raw, axis=0, keepdims=True), MP)
    grad_rms = jnp.sqrt(jnp.sum(squares) / (D // G * K) + 1e-06)
    grad_filters = raw * jnp.minimum(1.0, 1.0 / grad_rms)
    return (*forward, *backward, grad_filters)


def solution(mesh):
    fine = Mesh(mesh.devices.reshape(8, 2, 4, 4, 2), CTX + MP)
    placed = (P(CTX, MP), P(CTX, MP), P(CTX, MP), P(MP, None), P(CTX, MP))
    return jax.shard_map(
        shards,
        mesh=fine,
        in_specs=placed,
        out_specs=(P(CTX, MP), P(CTX, MP), P(CTX, MP), P(CTX, MP), P(MP, None)),
        check_vma=False,
    )
```

time: 77.8 us -> 73.2 us (0.941)
  waiting for transfers between devices: 12.3 us -> 5.56 us
  blocking collectives: 16.6 us -> 20.5 us
  Pallas kernels: 15 us -> 17 us
  starting transfers between devices: 23.7 us -> 21.8 us
  local copies, waits for them, and re-layouts: 4.29 us -> 2.66 us
    ppermute x1, waiting for transfers between devices: 6.4 us -> 0.01 us  [shards(): after = lax.ppermute(head, CTX, [(i + 1, i) for i in range(owners - 1)])]
    all_to_all x2, starting transfers between devices: 20.5 us -> 15.8 us  [sum_over(): lax.all_to_all(spread, axes, split_axis=0, concat_axis=0, tiled=True)]
    all_to_all x1, blocking collectives: 16.6 us -> 20.5 us  [sum_over(): lax.all_to_all(spread, axes, split_axis=0, concat_axis=0, tiled=True)]
    ppermute x1, starting transfers between devices: 1.85 us -> 4.59 us  [shards(): before = lax.ppermute(tail, CTX, [(i, i + 1) for i in range(owners - 1)])]
    pallas_call x2 -> x4, Pallas kernels: 15 us -> 17 us  [the longest x2 9.69 us: conv(): pl.pallas_call(functools.partial(conv_kernel, causal), in_specs=[HBM] * 4...]
    convert_element_type x2, other arithmetic: 1.17 us -> 2.2 us  [product_of(): (first.astype(jnp.float32) * second.astype(jnp.float32)).astype(jnp.bfloa...]
  transfers between devices with their start and end apart: 4 -> 4, of which waited for: 2 -> 2; matrix products, arithmetic and copies ran while one was open for 3% -> 2% of each run, Pallas kernels for 10% -> 23%
where the time goes in v2:
time: 73.2 us; the launch traced here: 72.7 us
  starting transfers between devices  21.8 us (30%)
  blocking collectives  20.5 us (28%)
  Pallas kernels  17 us (23%)
  waiting for transfers between devices  5.56 us (8%)
  other arithmetic  3.57 us (5%)
  local copies, waits for them, and re-layouts  2.66 us (4%)
  between operations  1.49 us (2%)
    all_to_all x1, blocking collectives, sum_over(): lax.all_to_all(spread, axes, split_axis=0, concat_axis=0, tiled=True)  20.5 us
    all_to_all x2, starting transfers between devices, sum_over(): lax.all_to_all(spread, axes, split_axis=0, concat_axis=0, tiled=True)  15.8 us
    pallas_call x2, Pallas kernels, conv(): pl.pallas_call(functools.partial(conv_kernel, causal), in_specs=[HBM] * 4...  9.69 us
    pallas_call x1, Pallas kernels, local_filter(): pl.pallas_call(local_kernel, in_specs=[HBM] * 4, out_specs=VMEM, out_shap...  5.66 us
    all_to_all x2, waiting for transfers between devices, sum_over(): lax.all_to_all(spread, axes, split_axis=0, concat_axis=0, tiled=True)  5.56 us
    ppermute x1, starting transfers between devices, shards(): before = lax.ppermute(tail, CTX, [(i, i + 1) for i in range(owners - 1)])  4.59 us
    convert_element_type x2, other arithmetic, product_of(): (first.astype(jnp.float32) * second.astype(jnp.float32)).astype(jnp.bfloa...  2.2 us
    pallas_call x1, Pallas kernels, edge_filter(): pl.pallas_call(edge_kernel, in_specs=[VMEM] * 3, out_specs=VMEM, out_shap...  1.68 us
  transfers between devices with their start and end apart: 4, of which 2 were waited for; matrix products, arithmetic and copies ran while one was open for 2% of the time, Pallas kernels for 23%

profile of v2, /device:TPU:1, one launch (start us, length us, event | category | flops | bytes accessed | tf_op | source)
XLA Modules:
  0.0 72.7 jit_solution(10726071085489467143)
XLA Ops:
  0.6 0.0 copy-start
  0.6 0.0 copy-start.2
  0.7 1.2 %multiply_convert_fusion = bf16[128,1024]{1,0:T(8,128)(2,1)S(1)} fusion(bf16[256,1024]{1,0:T(8,128)(2,1)} %b_hbm.3, bf16[256,1024]{1,0:T(8,128)(2,1)} %a_hbm.3), kind=kLoop, calls=%fused_computation | loop fusion | flops 524288 | bytes 786432 | tf_op jit(solution)/shard_map/convert_element_type | solution.py:26
  1.8 0.0 copy-start.1
  1.8 1.4 %collective-permute-start = (bf16[128,1024]{1,0:T(8,128)(2,1)S(1)}, bf16[128,1024]{1,0:T(8,128)(2,1)S(1)}, u32[]{:S(2)}, u32[]{:S(2)}) collective-permute-start(bf16[128,1024]{1,0:T(8,128)(2,1)S(1)} %multiply_convert_fusion), channel_id=1, source_target_pairs={{8,0},{16,8},{24,16},{32,24},{40,32},{48,40},{56,48},{64,56},{72,6... | collective-permute-start | bytes 786440 | tf_op jit(solution)/shard_map/ppermute | solution.py:209
  3.3 0.0 copy-done
  3.3 1.0 %multiply_convert_fusion.1.tail_ref = bf16[128,1024]{1,0:T(8,128)(2,1)S(1)} fusion(bf16[256,1024]{1,0:T(8,128)(2,1)} %x_hbm.3, bf16[256,1024]{1,0:T(8,128)(2,1)S(1)} %copy-done), kind=kLoop, calls=%fused_computation.1 | loop fusion | flops 524288 | bytes 786432 | tf_op jit(solution)/shard_map/convert_element_type | solution.py:26
  4.3 4.6 %collective-permute-start.1 = (bf16[128,1024]{1,0:T(8,128)(2,1)S(1)}, bf16[128,1024]{1,0:T(8,128)(2,1)S(1)}, u32[]{:S(2)}, u32[]{:S(2)}) collective-permute-start(bf16[128,1024]{1,0:T(8,128)(2,1)S(1)} %multiply_convert_fusion.1.tail_ref), channel_id=1, source_target_pairs={{0,8},{8,16},{16,24},{24,32},{32,40},{40,48},{48,56},{56,64},{64,7... | collective-permute-start | bytes 786440 | tf_op jit(solution)/shard_map/ppermute | solution.py:211
  8.9 0.0 copy-done.2
  8.9 0.0 copy-done.1
  8.9 0.0 copy-start.3
  8.9 1.0 %copy-done.3 = bf16[256,1024]{1,0:T(8,128)(2,1)S(1)} copy-done((bf16[256,1024]{1,0:T(8,128)(2,1)S(1)}, bf16[256,1024]{1,0:T(8,128)(2,1)}, u32[]{:S(2)}) %copy-start.3) | copy-done | bytes 524312
  10.0 5.7 %local_filter.1.local_ref = f32[64,128]{1,0:T(8,128)S(1)} custom-call(bf16[256,1024]{1,0:T(8,128)(2,1)S(1)} %copy-done.2, bf16[256,1024]{1,0:T(8,128)(2,1)S(1)} %copy-done, bf16[256,1024]{1,0:T(8,128)(2,1)S(1)} %copy-done.1, bf16[256,1024]{1,0:T(8,128)(2,1)S(1)} %copy-done.3), custom_call_target="tpu_custom_call" | custom-call | flops 3000000000 | bytes 2097152 | tf_op jit(solution)/shard_map/local_filter/pallas_call | solution.py:156
  15.6 0.0 collective-permute-done.after_ref.halo_ref
  15.7 1.7 %edge_filter.1 = f32[64,128]{1,0:T(8,128)S(1)} custom-call(bf16[128,1024]{1,0:T(8,128)(2,1)S(1)} %multiply_convert_fusion.1.tail_ref, bf16[128,1024]{1,0:T(8,128)(2,1)S(1)} %collective-permute-done.after_ref.halo_ref, f32[64,128]{1,0:T(8,128)S(1)} %local_filter.1.local_ref), custom_call_target="tpu_custom_call" | custom-call | flops 1000000000 | bytes 524288 | tf_op jit(solution)/shard_map/edge_filter/pallas_call | solution.py:170
  17.3 0.0 copy-start.4
  17.4 0.0 collective-permute-done.1.halo_ref
  17.4 0.7 broadcast_in_dim.6
  18.1 0.0 copy-start.5
  18.1 8.9 %all-to-all-start = ((f32[8,64,128]{2,1,0:T(8,128)}), f32[8,64,128]{2,1,0:T(8,128)S(1)}, u32[]{:S(2)}, u32[]{:S(2)}) async-start(f32[8,64,128]{2,1,0:T(8,128)} %broadcast_in_dim.6), calls=%async_computation | async-start | bytes 524288 | tf_op jit(solution)/shard_map/all_to_all | solution.py:201
  27.0 0.1 pad.3.clone
  27.1 0.0 copy-done.5
  27.1 0.1 rev.3
  27.2 0.1 maximum_maximum_fusion.filter_ref
  27.3 0.0 copy-done.4
  27.3 4.8 %forward_conv.1 = (bf16[256,1024]{1,0:T(8,128)(2,1)}, bf16[256,1024]{1,0:T(8,128)(2,1)}) custom-call(bf16[256,1024]{1,0:T(8,128)(2,1)S(1)} %copy-done, bf16[256,1024]{1,0:T(8,128)(2,1)S(1)} %copy-done.1, bf16[256,1024]{1,0:T(8,128)(2,1)S(1)} %copy-done.2, bf16[256,1024]{1,0:T(8,128)(2,1)S(1)} %copy-done.4, ...), custom_call_target="tpu_custom_call" | custom-call | flops 2000000000 | bytes 3145728 | tf_op jit(solution)/shard_map/forward_conv/pallas_call | solution.py:186
  32.1 1.0 %all-to-all-done = f32[8,64,128]{2,1,0:T(8,128)S(1)} async-done(((f32[8,64,128]{2,1,0:T(8,128)}), f32[8,64,128]{2,1,0:T(8,128)S(1)}, u32[]{:S(2)}, u32[]{:S(2)}) %all-to-all-start) | async-done | bytes 262176 | tf_op jit(solution)/shard_map/all_to_all | solution.py:201
  33.2 0.7 broadcast_in_dim.7
  33.9 6.9 %all-to-all-start.1 = ((f32[8,64,128]{2,1,0:T(8,128)}), f32[8,64,128]{2,1,0:T(8,128)S(1)}, u32[]{:S(2)}, u32[]{:S(2)}) async-start(f32[8,64,128]{2,1,0:T(8,128)} %broadcast_in_dim.7), calls=%async_computation.1 | async-start | bytes 524288 | tf_op jit(solution)/shard_map/all_to_all | solution.py:201
  40.7 4.9 %backward_conv.1 = (bf16[256,1024]{1,0:T(8,128)(2,1)}, bf16[256,1024]{1,0:T(8,128)(2,1)}) custom-call(bf16[256,1024]{1,0:T(8,128)(2,1)S(1)} %copy-done.4, bf16[256,1024]{1,0:T(8,128)(2,1)S(1)} %copy-done.2, bf16[256,1024]{1,0:T(8,128)(2,1)S(1)} %copy-done.1, bf16[256,1024]{1,0:T(8,128)(2,1)S(1)} %copy-done, ...), custom_call_target="tpu_custom_call" | custom-call | flops 2000000000 | bytes 3145728 | tf_op jit(solution)/shard_map/backward_conv/pallas_call | solution.py:186
  45.6 4.5 %all-to-all-done.1 = f32[8,64,128]{2,1,0:T(8,128)S(1)} async-done(((f32[8,64,128]{2,1,0:T(8,128)}), f32[8,64,128]{2,1,0:T(8,128)S(1)}, u32[]{:S(2)}, u32[]{:S(2)}) %all-to-all-start.1) | async-done | bytes 262176 | tf_op jit(solution)/shard_map/all_to_all | solution.py:201
  50.2 20.5 %all_to_all.15 = f32[8,1,128]{2,1,0:T(1,128)S(1)} all-to-all(f32[8,1,128]{2,1,0:T(1,128)S(1)} %broadcast_in_dim.8), channel_id=1, replica_groups=mesh['y'=8,'zl'=2,'x'=4,'zh'=4,'core'=2] {'zh','core'}, dimensions={0} | all-to-all | bytes 8192 | tf_op jit(solution)/shard_map/all_to_all | solution.py:201
  70.8 0.6 reduce_sum.43
  72.0 0.6 broadcast_multiply_fusion
  (7 shorter events, 0.1 us)
Async XLA Ops:
  0.6 2.7 %copy-start = (bf16[256,1024]{1,0:T(8,128)(2,1)S(1)}, bf16[256,1024]{1,0:T(8,128)(2,1)}, u32[]{:S(2)}) copy-start(bf16[256,1024]{1,0:T(8,128)(2,1)} %y_hbm.3) | copy-start | bytes 1572868
  0.6 8.3 %copy-start.2 = (bf16[256,1024]{1,0:T(8,128)(2,1)S(1)}, bf16[256,1024]{1,0:T(8,128)(2,1)}, u32[]{:S(2)}) copy-start(bf16[256,1024]{1,0:T(8,128)(2,1)} %b_hbm.3) | copy-start | bytes 1572868
  1.8 7.1 %copy-start.1 = (bf16[256,1024]{1,0:T(8,128)(2,1)S(1)}, bf16[256,1024]{1,0:T(8,128)(2,1)}, u32[]{:S(2)}) copy-start(bf16[256,1024]{1,0:T(8,128)(2,1)} %x_hbm.3) | copy-start | bytes 1572868
  1.8 13.8 %collective-permute-start = (bf16[128,1024]{1,0:T(8,128)(2,1)S(1)}, bf16[128,1024]{1,0:T(8,128)(2,1)S(1)}, u32[]{:S(2)}, u32[]{:S(2)}) collective-permute-start(bf16[128,1024]{1,0:T(8,128)(2,1)S(1)} %multiply_convert_fusion), channel_id=1, source_target_pairs={{8,0},{16,8},{24,16},{32,24},{40,32},{48,40},{56,48},{64,56},{72,6... | collective-permute-start | bytes 786440 | tf_op jit(solution)/shard_map/ppermute | solution.py:209
  4.3 13.0 %collective-permute-start.1 = (bf16[128,1024]{1,0:T(8,128)(2,1)S(1)}, bf16[128,1024]{1,0:T(8,128)(2,1)S(1)}, u32[]{:S(2)}, u32[]{:S(2)}) collective-permute-start(bf16[128,1024]{1,0:T(8,128)(2,1)S(1)} %multiply_convert_fusion.1.tail_ref), channel_id=1, source_target_pairs={{0,8},{8,16},{16,24},{24,32},{32,40},{40,48},{48,56},{56,64},{64,7... | collective-permute-start | bytes 786440 | tf_op jit(solution)/shard_map/ppermute | solution.py:211
  8.9 1.0 %copy-start.3 = (bf16[256,1024]{1,0:T(8,128)(2,1)S(1)}, bf16[256,1024]{1,0:T(8,128)(2,1)}, u32[]{:S(2)}) copy-start(bf16[256,1024]{1,0:T(8,128)(2,1)} %a_hbm.3) | copy-start | bytes 1572868
  17.3 9.9 %copy-start.4 = (bf16[256,1024]{1,0:T(8,128)(2,1)S(1)}, bf16[256,1024]{1,0:T(8,128)(2,1)}, u32[]{:S(2)}) copy-start(bf16[256,1024]{1,0:T(8,128)(2,1)} %a_hbm.3) | copy-start | bytes 1572868
  18.1 9.0 %copy-start.5 = (bf16[64,128]{1,0:T(8,128)(2,1)S(1)}, bf16[64,128]{1,0:T(8,128)(2,1)}, u32[]{:S(2)}) copy-start(bf16[64,128]{1,0:T(8,128)(2,1)} %param.8) | copy-start | bytes 49156
  18.1 15.0 %all-to-all-start = ((f32[8,64,128]{2,1,0:T(8,128)}), f32[8,64,128]{2,1,0:T(8,128)S(1)}, u32[]{:S(2)}, u32[]{:S(2)}) async-start(f32[8,64,128]{2,1,0:T(8,128)} %broadcast_in_dim.6), calls=%async_computation | async-start | bytes 524288 | tf_op jit(solution)/shard_map/all_to_all | solution.py:201
  33.9 16.3 %all-to-all-start.1 = ((f32[8,64,128]{2,1,0:T(8,128)}), f32[8,64,128]{2,1,0:T(8,128)S(1)}, u32[]{:S(2)}, u32[]{:S(2)}) async-start(f32[8,64,128]{2,1,0:T(8,128)} %broadcast_in_dim.7), calls=%async_computation.1 | async-start | bytes 524288 | tf_op jit(solution)/shard_map/all_to_all | solution.py:201

commit v3 on v2

v3 whole, which is shorter than its diff:
```python
import functools

import jax
import jax.numpy as jnp
from jax import lax
from jax.experimental import pallas as pl
from jax.experimental.pallas import tpu as pltpu
from jax.sharding import Mesh, PartitionSpec as P

D = 8192
G = 16
K = 128
B = 16
FB = 32
W = 2 * K
LANES = 128
UNROLL = 4
LIMIT = 8 << 20
TILE_GROUPS = LANES // G
CTX = ("y", "zl", "x")
MP = ("zh", "core")
HBM = pl.BlockSpec(memory_space=pl.ANY)
VMEM = pl.BlockSpec(memory_space=pltpu.VMEM)


def product_of(first, second):
    return (first.astype(jnp.float32) * second.astype(jnp.float32)).astype(jnp.bfloat16)


def blocks_of(rows, size):
    return jnp.concatenate([rows[n : n + size] for n in range(0, rows.shape[0], size)], axis=1)


def windows(rows, size):
    return jnp.concatenate([rows[n : n + W] for n in range(0, rows.shape[0] - W + size, size)], axis=1)


def group_of_lane(shape):
    return (lax.broadcasted_iota(jnp.int32, shape, 1) % LANES) // G


def correlate(product, following, tile, rows_ref):
    left = blocks_of(product, FB)
    group = group_of_lane(left.shape)
    zero = jnp.zeros_like(left)
    left = jnp.concatenate([jnp.where(group == g, left, zero) for g in range(TILE_GROUPS)], axis=0)
    pad = jnp.zeros((product.shape[0] - FB + W - following.shape[0], LANES), jnp.bfloat16)
    wins = windows(jnp.concatenate([following, pad], axis=0), FB)
    pairs = lax.dot_general(left, wins, (((1,), (1,)), ((), ())), preferred_element_type=jnp.float32)
    for g in range(TILE_GROUPS):
        total = pairs[g * FB : g * FB + 8]
        for r in range(8, FB, 8):
            total = total + pltpu.roll(pairs[g * FB + r : g * FB + r + 8], W - r, 1)
        rows_ref[pl.ds((tile * TILE_GROUPS + g) * 8, 8), :] = total


def fold(rows_ref):
    rows = rows_ref[...]
    sub = lax.broadcasted_iota(jnp.int32, rows.shape, 0)
    for bit in (1, 2, 4):
        rows = jnp.where((sub & bit) != 0, pltpu.roll(rows, W - bit, 1), rows)
    return jnp.sum(rows[:, :K].reshape(rows.shape[0] // 8, 8, K), axis=1)


def lanes_of(tile):
    return pl.ds(pl.multiple_of(tile * LANES, LANES), LANES)


def local_kernel(q_ref, k_ref, v_ref, go_ref, raw_ref, tail_ref, rows):
    tokens = q_ref.shape[0]

    @pl.loop(0, q_ref.shape[1] // LANES, unroll=UNROLL)
    def _(t):
        c = lanes_of(t)
        product = product_of(k_ref[:, c], v_ref[:, c])
        tail_ref[:, c] = product[tokens - K :]
        correlate(product, product_of(go_ref[:, c], q_ref[:, c]), t, rows)

    raw_ref[...] = fold(rows)


def edge_kernel(tail_ref, after_ref, local_ref, raw_ref, rows):
    @pl.loop(0, tail_ref.shape[1] // LANES, unroll=UNROLL)
    def _(t):
        c = lanes_of(t)
        following = jnp.concatenate([jnp.zeros((K, LANES), jnp.bfloat16), after_ref[:, c]], axis=0)
        correlate(tail_ref[:, c], following, t, rows)

    raw_ref[...] = local_ref[...] + fold(rows)


def scale_kernel(raw_ref, squares_ref, out_ref):
    raw = raw_ref[...]
    mean = jnp.sum(squares_ref[...], axis=(0, 1), keepdims=True)[0]
    mean = jnp.sum(mean, axis=1, keepdims=True) / (D // G * K)
    out_ref[...] = raw * jnp.minimum(1.0, 1.0 / jnp.sqrt(mean + 1e-06))


def toeplitz_rows(rows_ref, t):
    mats = []
    for g in range(TILE_GROUPS):
        row = jnp.broadcast_to(rows_ref[pl.ds(t * TILE_GROUPS + g, 1), :], (B, W))
        mats.append(pltpu.roll(row, 0, 1, stride=1, stride_axis=0).astype(jnp.bfloat16))
    return jnp.concatenate(mats, axis=0)


def convolve(mats, rows):
    blocks = (rows.shape[0] - K) // B
    pad = jnp.zeros((W - K - B, LANES), jnp.bfloat16)
    wins = windows(jnp.concatenate([rows, pad], axis=0), B)
    full = jnp.dot(mats, wins, preferred_element_type=jnp.float32)
    group = group_of_lane((B, blocks * LANES))
    total = full[:B]
    for g in range(1, TILE_GROUPS):
        total = jnp.where(group == g, full[g * B : (g + 1) * B], total)
    total = total.astype(jnp.bfloat16).astype(jnp.float32)
    return jnp.concatenate([total[:, n * LANES : (n + 1) * LANES] for n in range(blocks)], axis=0)


def conv_kernel(causal, a_ref, b_ref, x_ref, y_ref, halo_ref, filter_ref, ox_hbm, oy_hbm, ox_buf, oy_buf, sems):
    tiles = a_ref.shape[1] // LANES

    def copies_of(t):
        c = lanes_of(t)
        pairs = ((ox_buf, ox_hbm), (oy_buf, oy_hbm))
        return [pltpu.make_async_copy(src.at[:, c], dst.at[:, c], sems.at[n, t]) for n, (src, dst) in enumerate(pairs)]

    @pl.loop(0, tiles, unroll=2)
    def _(t):
        c = lanes_of(t)
        own, halo = product_of(a_ref[:, c], b_ref[:, c]), halo_ref[:, c]
        out = convolve(toeplitz_rows(filter_ref, t), jnp.concatenate([halo, own] if causal else [own, halo], axis=0))
        ox_buf[:, c] = (out * x_ref[:, c].astype(jnp.float32)).astype(jnp.bfloat16)
        oy_buf[:, c] = (out * y_ref[:, c].astype(jnp.float32)).astype(jnp.bfloat16)
        for copy in copies_of(t):
            copy.start()

    @pl.loop(0, tiles)
    def _(t):
        for copy in copies_of(t):
            copy.wait()


def local_filter(q, k, v, go, slab_groups):
    return pl.pallas_call(
        local_kernel,
        in_specs=[VMEM] * 4,
        out_specs=[VMEM] * 2,
        out_shape=[
            jax.ShapeDtypeStruct((slab_groups, K), jnp.float32),
            jax.ShapeDtypeStruct((K, q.shape[1]), jnp.bfloat16),
        ],
        scratch_shapes=[pltpu.VMEM((slab_groups * 8, W), jnp.float32)],
        cost_estimate=pl.CostEstimate(flops=3 * 10**9, bytes_accessed=2**21, transcendentals=0),
        compiler_params=pltpu.CompilerParams(vmem_limit_bytes=LIMIT),
        name="local_filter",
    )(q, k, v, go)


def edge_filter(tail, after, local):
    return pl.pallas_call(
        edge_kernel,
        in_specs=[VMEM] * 3,
        out_specs=VMEM,
        out_shape=jax.ShapeDtypeStruct(local.shape, jnp.float32),
        scratch_shapes=[pltpu.VMEM((local.shape[0] * 8, W), jnp.float32)],
        cost_estimate=pl.CostEstimate(flops=10**9, bytes_accessed=2**19, transcendentals=0),
        compiler_params=pltpu.CompilerParams(vmem_limit_bytes=LIMIT),
        name="edge_filter",
    )(tail, after, local)


def conv(causal, signal, factors, halo, filter_rows):
    wide = jax.ShapeDtypeStruct(signal[0].shape, jnp.bfloat16)
    return pl.pallas_call(
        functools.partial(conv_kernel, causal),
        in_specs=[VMEM] * 6,
        out_specs=[HBM] * 2,
        out_shape=[wide] * 2,
        scratch_shapes=[pltpu.VMEM(wide.shape, jnp.bfloat16)] * 2
        + [pltpu.SemaphoreType.DMA((2, wide.shape[1] // LANES))],
        cost_estimate=pl.CostEstimate(flops=2 * 10**9, bytes_accessed=3 * 2**20, transcendentals=0),
        compiler_params=pltpu.CompilerParams(vmem_limit_bytes=LIMIT),
        name="forward_conv" if causal else "backward_conv",
    )(*signal, *factors, halo, filter_rows)


def scale(raw, squares):
    return pl.pallas_call(
        scale_kernel,
        in_specs=[VMEM] * 2,
        out_specs=VMEM,
        out_shape=jax.ShapeDtypeStruct(raw.shape, jnp.float32),
        compiler_params=pltpu.CompilerParams(vmem_limit_bytes=LIMIT),
        name="scale",
    )(raw, squares)


def spread_over(value, axes):
    size = lax.axis_size(axes)
    spread = jnp.broadcast_to(value[None], (size,) + value.shape)
    return lax.all_to_all(spread, axes, split_axis=0, concat_axis=0, tiled=True)


def shards(queries, key_feats, value_feats, filters, grad_out):
    slab_groups = filters.shape[0]
    owners = lax.axis_size(CTX)
    head = product_of(grad_out[:K], queries[:K])
    after = lax.ppermute(head, CTX, [(i + 1, i) for i in range(owners - 1)])
    local, tail = local_filter(queries, key_feats, value_feats, grad_out, slab_groups)
    raw = edge_filter(tail, after, local)

    filt = filters.astype(jnp.float32)
    zeros = jnp.zeros((slab_groups, W - K), jnp.float32)
    backward_rows = jnp.concatenate([filt, zeros], axis=1)
    forward_rows = jnp.concatenate([zeros[:, :1], filt[:, ::-1], zeros[:, 1:]], axis=1)

    raw, tail, after = lax.optimization_barrier((raw, tail, after))
    before = lax.ppermute(tail, CTX, [(i, i + 1) for i in range(owners - 1)])
    backward = conv(False, (grad_out, queries), (value_feats, key_feats), after, backward_rows)
    raw = jnp.sum(spread_over(raw, ("zl", "x")), axis=0)
    raw, before, backward = lax.optimization_barrier((raw, before, backward))
    forward = conv(True, (key_feats, value_feats), (queries, grad_out), before, forward_rows)
    raw = jnp.sum(spread_over(raw, ("y",)), axis=0)
    raw, forward = lax.optimization_barrier((raw, forward))
    grad_filters = scale(raw, spread_over(jnp.sum(raw * raw, axis=0, keepdims=True), MP))
    return (*forward, *backward, grad_filters)


def solution(mesh):
    fine = Mesh(mesh.devices.reshape(8, 2, 4, 4, 2), CTX + MP)
    placed = (P(CTX, MP), P(CTX, MP), P(CTX, MP), P(MP, None), P(CTX, MP))
    return jax.shard_map(
        shards,
        mesh=fine,
        in_specs=placed,
        out_specs=(P(CTX, MP), P(CTX, MP), P(CTX, MP), P(CTX, MP), P(MP, None)),
        check_vma=False,
    )
```

time: 73.2 us -> 73.5 us (level)
  Pallas kernels: 17 us -> 10.3 us
  starting transfers between devices: 21.8 us -> 26.2 us
  waiting for transfers between devices: 5.56 us -> 9.3 us
  other arithmetic: 3.57 us -> 1.3 us
  local copies, waits for them, and re-layouts: 2.66 us -> 4.75 us
    pallas_call x3 -> x4, Pallas kernels: 15.4 us -> 8.6 us  [the longest x2 5.6 us: conv(): pl.pallas_call(functools.partial(conv_kernel, causal), in_specs=[VMEM] *...]
    all_to_all x2, starting transfers between devices: 15.8 us -> 21.5 us  [spread_over(): return lax.all_to_all(spread, axes, split_axis=0, concat_axis=0, tiled=True)]
    unnamed x12 -> x16, local copies, waits for them, and re-layouts: 1.06 us -> 3.14 us
    ppermute x1, waiting for transfers between devices: 0.01 us -> 1.95 us  [shards(): before = lax.ppermute(tail, CTX, [(i, i + 1) for i in range(owners - 1)])]
    ppermute x1, starting transfers between devices: 4.59 us -> 3.37 us  [shards(): before = lax.ppermute(tail, CTX, [(i, i + 1) for i in range(owners - 1)])]
    convert_element_type x2 -> x1, other arithmetic: 2.2 us -> 1.15 us  [product_of(): (first.astype(jnp.float32) * second.astype(jnp.float32)).astype(jnp.bfloa...]
    ppermute x1, waiting for transfers between devices: 0.01 us -> 0.98 us  [shards(): after = lax.ppermute(head, CTX, [(i + 1, i) for i in range(owners - 1)])]
    all_to_all x2, waiting for transfers between devices: 5.56 us -> 6.38 us  [spread_over(): return lax.all_to_all(spread, axes, split_axis=0, concat_axis=0, tiled=True)]
  transfers between devices with their start and end apart: 4 -> 4, of which waited for: 2 -> 3; matrix products, arithmetic and copies ran while one was open for 2% -> 0% of each run, Pallas kernels for 23% -> 11%
where the time goes in v3:
time: 73.5 us; the launch traced here: 72.9 us
  starting transfers between devices  26.2 us (36%)
  blocking collectives  20.3 us (28%)
  Pallas kernels  10.3 us (14%)
  waiting for transfers between devices  9.3 us (13%)
  local copies, waits for them, and re-layouts  4.75 us (6%)
  other arithmetic  1.3 us (2%)
  between operations  0.79 us (1%)
    all_to_all x2, starting transfers between devices, spread_over(): return lax.all_to_all(spread, axes, split_axis=0, concat_axis=0, tiled=True)  21.5 us
    all_to_all x1, blocking collectives, spread_over(): return lax.all_to_all(spread, axes, split_axis=0, concat_axis=0, tiled=True)  20.3 us
    all_to_all x2, waiting for transfers between devices, spread_over(): return lax.all_to_all(spread, axes, split_axis=0, concat_axis=0, tiled=True)  6.38 us
    pallas_call x2, Pallas kernels, conv(): pl.pallas_call(functools.partial(conv_kernel, causal), in_specs=[VMEM] *...  5.6 us
    ppermute x1, starting transfers between devices, shards(): before = lax.ppermute(tail, CTX, [(i, i + 1) for i in range(owners - 1)])  3.37 us
    unnamed x16, local copies, waits for them, and re-layouts  3.14 us
    pallas_call x1, Pallas kernels, local_filter(): pl.pallas_call(local_kernel, in_specs=[VMEM] * 4, out_specs=[VMEM] * 2, o...  2.28 us
    ppermute x1, waiting for transfers between devices, shards(): before = lax.ppermute(tail, CTX, [(i, i + 1) for i in range(owners - 1)])  1.95 us
  transfers between devices with their start and end apart: 4, of which 3 were waited for; matrix products, arithmetic and copies ran while one was open for 0% of the time, Pallas kernels for 11%

profile of v3, /device:TPU:1, one launch (start us, length us, event | category | flops | bytes accessed | tf_op | source)
XLA Modules:
  0.0 72.9 jit_solution(4636402546288334907)
XLA Ops:
  0.6 0.0 copy-start
  0.6 1.2 %multiply_convert_fusion = bf16[128,1024]{1,0:T(8,128)(2,1)S(1)} fusion(bf16[256,1024]{1,0:T(8,128)(2,1)} %x_ref.3, bf16[256,1024]{1,0:T(8,128)(2,1)} %y_ref.3), kind=kLoop, calls=%fused_computation | loop fusion | flops 524288 | bytes 786432 | tf_op jit(solution)/shard_map/convert_element_type | solution.py:27
  1.8 1.3 %collective-permute-start = (bf16[128,1024]{1,0:T(8,128)(2,1)S(1)}, bf16[128,1024]{1,0:T(8,128)(2,1)S(1)}, u32[]{:S(2)}, u32[]{:S(2)}) collective-permute-start(bf16[128,1024]{1,0:T(8,128)(2,1)S(1)} %multiply_convert_fusion), channel_id=1, source_target_pairs={{8,0},{16,8},{24,16},{32,24},{40,32},{48,40},{56,48},{64,56},{72,6... | collective-permute-start | bytes 786440 | tf_op jit(solution)/shard_map/ppermute | solution.py:209
  3.1 0.0 copy-done
  3.1 0.0 copy-start.1
  3.1 1.0 %copy-done.1 = bf16[256,1024]{1,0:T(8,128)(2,1)S(1)} copy-done((bf16[256,1024]{1,0:T(8,128)(2,1)S(1)}, bf16[256,1024]{1,0:T(8,128)(2,1)}, u32[]{:S(2)}) %copy-start.1) | copy-done | bytes 524312
  4.2 0.0 copy-start.3
  4.2 1.0 %copy-done.3 = bf16[256,1024]{1,0:T(8,128)(2,1)S(1)} copy-done((bf16[256,1024]{1,0:T(8,128)(2,1)S(1)}, bf16[256,1024]{1,0:T(8,128)(2,1)}, u32[]{:S(2)}) %copy-start.3) | copy-done | bytes 524312
  5.2 0.0 copy-start.5
  5.2 1.0 %copy-done.5 = bf16[256,1024]{1,0:T(8,128)(2,1)S(1)} copy-done((bf16[256,1024]{1,0:T(8,128)(2,1)S(1)}, bf16[256,1024]{1,0:T(8,128)(2,1)}, u32[]{:S(2)}) %copy-start.5) | copy-done | bytes 524312
  6.2 2.3 %local_filter.1 = (f32[64,128]{1,0:T(8,128)S(1)}, bf16[128,1024]{1,0:T(8,128)(2,1)S(1)}) custom-call(bf16[256,1024]{1,0:T(8,128)(2,1)S(1)} %copy-done, bf16[256,1024]{1,0:T(8,128)(2,1)S(1)} %copy-done.3, bf16[256,1024]{1,0:T(8,128)(2,1)S(1)} %copy-done.5, bf16[256,1024]{1,0:T(8,128)(2,1)S(1)} %copy-done.1), custom_call_target="tpu_custom_call" | custom-call | flops 3000000000 | bytes 2097152 | tf_op jit(solution)/shard_map/local_filter/pallas_call | solution.py:145
  8.5 1.0 %collective-permute-done.after_ref.halo_ref = bf16[128,1024]{1,0:T(8,128)(2,1)S(1)} collective-permute-done((bf16[128,1024]{1,0:T(8,128)(2,1)S(1)}, bf16[128,1024]{1,0:T(8,128)(2,1)S(1)}, u32[]{:S(2)}, u32[]{:S(2)}) %collective-permute-start) | collective-permute-done | bytes 262176 | tf_op jit(solution)/shard_map/ppermute | solution.py:209
  9.5 0.0 copy-start.4
  9.5 0.0 copy-start.6
  9.5 1.7 %edge_filter.1 = f32[64,128]{1,0:T(8,128)S(1)} custom-call(bf16[128,1024]{1,0:T(8,128)(2,1)S(1)} %get-tuple-element.24.tail_ref, bf16[128,1024]{1,0:T(8,128)(2,1)S(1)} %collective-permute-done.after_ref.halo_ref, f32[64,128]{1,0:T(8,128)S(1)} %get-tuple-element.22.local_ref), custom_call_target="tpu_custom_call" | custom-call | flops 1000000000 | bytes 524288 | tf_op jit(solution)/shard_map/edge_filter/pallas_call | solution.py:161
  11.2 0.0 copy-start.2
  11.2 0.7 broadcast_in_dim.6
  11.9 0.0 copy-start.7
  11.9 10.9 %all-to-all-start = ((f32[8,64,128]{2,1,0:T(8,128)}), f32[8,64,128]{2,1,0:T(8,128)S(1)}, u32[]{:S(2)}, u32[]{:S(2)}) async-start(f32[8,64,128]{2,1,0:T(8,128)} %broadcast_in_dim.6), calls=%async_computation | async-start | bytes 524288 | tf_op jit(solution)/shard_map/all_to_all | solution.py:202
  22.8 3.4 %collective-permute-start.1 = (bf16[128,1024]{1,0:T(8,128)(2,1)S(1)}, bf16[128,1024]{1,0:T(8,128)(2,1)S(1)}, u32[]{:S(2)}, u32[]{:S(2)}) collective-permute-start(bf16[128,1024]{1,0:T(8,128)(2,1)S(1)} %get-tuple-element.24.tail_ref), channel_id=1, source_target_pairs={{0,8},{8,16},{16,24},{24,32},{32,40},{40,48},{48,56},{56,64},{64,7... | collective-permute-start | bytes 786440 | tf_op jit(solution)/shard_map/ppermute | solution.py:219
  26.2 0.0 copy-done.7
  26.2 0.0 copy-done.4
  26.2 0.0 copy-done.6
  26.2 0.0 copy-done.2
  26.3 2.8 %backward_conv.1 = (bf16[256,1024]{1,0:T(8,128)(2,1)}, bf16[256,1024]{1,0:T(8,128)(2,1)}) custom-call(bf16[256,1024]{1,0:T(8,128)(2,1)S(1)} %copy-done.2, bf16[256,1024]{1,0:T(8,128)(2,1)S(1)} %copy-done, bf16[256,1024]{1,0:T(8,128)(2,1)S(1)} %copy-done.6, bf16[256,1024]{1,0:T(8,128)(2,1)S(1)} %copy-done.4, ...), custom_call_target="tpu_custom_call" | custom-call | flops 2000000000 | bytes 3145728 | tf_op jit(solution)/shard_map/backward_conv/pallas_call | solution.py:175
  29.1 0.0 all-to-all-done
  29.1 1.9 %collective-permute-done.1.halo_ref = bf16[128,1024]{1,0:T(8,128)(2,1)S(1)} collective-permute-done((bf16[128,1024]{1,0:T(8,128)(2,1)S(1)}, bf16[128,1024]{1,0:T(8,128)(2,1)S(1)}, u32[]{:S(2)}, u32[]{:S(2)}) %collective-permute-start.1) | collective-permute-done | bytes 262176 | tf_op jit(solution)/shard_map/ppermute | solution.py:219
  31.1 0.7 broadcast_in_dim.7
  31.8 10.6 %all-to-all-start.1 = ((f32[8,64,128]{2,1,0:T(8,128)}), f32[8,64,128]{2,1,0:T(8,128)S(1)}, u32[]{:S(2)}, u32[]{:S(2)}) async-start(f32[8,64,128]{2,1,0:T(8,128)} %broadcast_in_dim.7), calls=%async_computation.1 | async-start | bytes 524288 | tf_op jit(solution)/shard_map/all_to_all | solution.py:202
  42.4 0.1 rev.3
  42.5 0.1 pad.3.clone
  42.6 0.1 maximum_maximum_fusion.filter_ref
  42.7 2.8 %forward_conv.1 = (bf16[256,1024]{1,0:T(8,128)(2,1)}, bf16[256,1024]{1,0:T(8,128)(2,1)}) custom-call(bf16[256,1024]{1,0:T(8,128)(2,1)S(1)} %copy-done.4, bf16[256,1024]{1,0:T(8,128)(2,1)S(1)} %copy-done.6, bf16[256,1024]{1,0:T(8,128)(2,1)S(1)} %copy-done, bf16[256,1024]{1,0:T(8,128)(2,1)S(1)} %copy-done.2, ...), custom_call_target="tpu_custom_call" | custom-call | flops 2000000000 | bytes 3145728 | tf_op jit(solution)/shard_map/forward_conv/pallas_call | solution.py:175
  45.5 6.4 %all-to-all-done.1 = f32[8,64,128]{2,1,0:T(8,128)S(1)} async-done(((f32[8,64,128]{2,1,0:T(8,128)}), f32[8,64,128]{2,1,0:T(8,128)S(1)}, u32[]{:S(2)}, u32[]{:S(2)}) %all-to-all-start.1) | async-done | bytes 262176 | tf_op jit(solution)/shard_map/all_to_all | solution.py:202
  51.9 20.3 %all_to_all.15.squares_ref = f32[8,1,128]{2,1,0:T(1,128)S(1)} all-to-all(f32[8,1,128]{2,1,0:T(1,128)S(1)} %broadcast_in_dim.8), channel_id=1, replica_groups=mesh['y'=8,'zl'=2,'x'=4,'zh'=4,'core'=2] {'zh','core'}, dimensions={0} | all-to-all | bytes 8192 | tf_op jit(solution)/shard_map/all_to_all | solution.py:202
  72.2 0.7 scale.1
  (7 shorter events, 0.1 us)
Async XLA Ops:
  0.6 2.5 %copy-start = (bf16[256,1024]{1,0:T(8,128)(2,1)S(1)}, bf16[256,1024]{1,0:T(8,128)(2,1)}, u32[]{:S(2)}) copy-start(bf16[256,1024]{1,0:T(8,128)(2,1)} %x_ref.3) | copy-start | bytes 1572868
  1.8 7.7 %collective-permute-start = (bf16[128,1024]{1,0:T(8,128)(2,1)S(1)}, bf16[128,1024]{1,0:T(8,128)(2,1)S(1)}, u32[]{:S(2)}, u32[]{:S(2)}) collective-permute-start(bf16[128,1024]{1,0:T(8,128)(2,1)S(1)} %multiply_convert_fusion), channel_id=1, source_target_pairs={{8,0},{16,8},{24,16},{32,24},{40,32},{48,40},{56,48},{64,56},{72,6... | collective-permute-start | bytes 786440 | tf_op jit(solution)/shard_map/ppermute | solution.py:209
  3.1 1.0 %copy-start.1 = (bf16[256,1024]{1,0:T(8,128)(2,1)S(1)}, bf16[256,1024]{1,0:T(8,128)(2,1)}, u32[]{:S(2)}) copy-start(bf16[256,1024]{1,0:T(8,128)(2,1)} %y_ref.3) | copy-start | bytes 1572868
  4.2 1.0 %copy-start.3 = (bf16[256,1024]{1,0:T(8,128)(2,1)S(1)}, bf16[256,1024]{1,0:T(8,128)(2,1)}, u32[]{:S(2)}) copy-start(bf16[256,1024]{1,0:T(8,128)(2,1)} %a_ref.3) | copy-start | bytes 1572868
  5.2 1.0 %copy-start.5 = (bf16[256,1024]{1,0:T(8,128)(2,1)S(1)}, bf16[256,1024]{1,0:T(8,128)(2,1)}, u32[]{:S(2)}) copy-start(bf16[256,1024]{1,0:T(8,128)(2,1)} %b_ref.3) | copy-start | bytes 1572868
  9.5 16.7 %copy-start.4 = (bf16[256,1024]{1,0:T(8,128)(2,1)S(1)}, bf16[256,1024]{1,0:T(8,128)(2,1)}, u32[]{:S(2)}) copy-start(bf16[256,1024]{1,0:T(8,128)(2,1)} %a_ref.3) | copy-start | bytes 1572868
  9.5 16.7 %copy-start.6 = (bf16[256,1024]{1,0:T(8,128)(2,1)S(1)}, bf16[256,1024]{1,0:T(8,128)(2,1)}, u32[]{:S(2)}) copy-start(bf16[256,1024]{1,0:T(8,128)(2,1)} %b_ref.3) | copy-start | bytes 1572868
  11.2 15.1 %copy-start.2 = (bf16[256,1024]{1,0:T(8,128)(2,1)S(1)}, bf16[256,1024]{1,0:T(8,128)(2,1)}, u32[]{:S(2)}) copy-start(bf16[256,1024]{1,0:T(8,128)(2,1)} %y_ref.3) | copy-start | bytes 1572868
  11.9 14.3 %copy-start.7 = (bf16[64,128]{1,0:T(8,128)(2,1)S(1)}, bf16[64,128]{1,0:T(8,128)(2,1)}, u32[]{:S(2)}) copy-start(bf16[64,128]{1,0:T(8,128)(2,1)} %param.8) | copy-start | bytes 49156
  11.9 17.2 %all-to-all-start = ((f32[8,64,128]{2,1,0:T(8,128)}), f32[8,64,128]{2,1,0:T(8,128)S(1)}, u32[]{:S(2)}, u32[]{:S(2)}) async-start(f32[8,64,128]{2,1,0:T(8,128)} %broadcast_in_dim.6), calls=%async_computation | async-start | bytes 524288 | tf_op jit(solution)/shard_map/all_to_all | solution.py:202
  22.8 8.2 %collective-permute-start.1 = (bf16[128,1024]{1,0:T(8,128)(2,1)S(1)}, bf16[128,1024]{1,0:T(8,128)(2,1)S(1)}, u32[]{:S(2)}, u32[]{:S(2)}) collective-permute-start(bf16[128,1024]{1,0:T(8,128)(2,1)S(1)} %get-tuple-element.24.tail_ref), channel_id=1, source_target_pairs={{0,8},{8,16},{16,24},{24,32},{32,40},{40,48},{48,56},{56,64},{64,7... | collective-permute-start | bytes 786440 | tf_op jit(solution)/shard_map/ppermute | solution.py:219
  31.8 20.1 %all-to-all-start.1 = ((f32[8,64,128]{2,1,0:T(8,128)}), f32[8,64,128]{2,1,0:T(8,128)S(1)}, u32[]{:S(2)}, u32[]{:S(2)}) async-start(f32[8,64,128]{2,1,0:T(8,128)} %broadcast_in_dim.7), calls=%async_computation.1 | async-start | bytes 524288 | tf_op jit(solution)/shard_map/all_to_all | solution.py:202

commit v4 on v3

--- a/solution.py
+++ b/solution.py
@@ -179,7 +179,7 @@
         out_shape=[wide] * 2,
         scratch_shapes=[pltpu.VMEM(wide.shape, jnp.bfloat16)] * 2
         + [pltpu.SemaphoreType.DMA((2, wide.shape[1] // LANES))],
-        cost_estimate=pl.CostEstimate(flops=2 * 10**9, bytes_accessed=3 * 2**20, transcendentals=0),
+        cost_estimate=pl.CostEstimate(flops=10**10, bytes_accessed=3 * 2**20, transcendentals=0),
         compiler_params=pltpu.CompilerParams(vmem_limit_bytes=LIMIT),
         name="forward_conv" if causal else "backward_conv",
     )(*signal, *factors, halo, filter_rows)
@@ -215,11 +215,12 @@
     backward_rows = jnp.concatenate([filt, zeros], axis=1)
     forward_rows = jnp.concatenate([zeros[:, :1], filt[:, ::-1], zeros[:, 1:]], axis=1)
 
-    raw, tail, after = lax.optimization_barrier((raw, tail, after))
     before = lax.ppermute(tail, CTX, [(i, i + 1) for i in range(owners - 1)])
+    before, after, _ = lax.optimization_barrier((before, after, raw))
     backward = conv(False, (grad_out, queries), (value_feats, key_feats), after, backward_rows)
     raw = jnp.sum(spread_over(raw, ("zl", "x")), axis=0)
-    raw, before, backward = lax.optimization_barrier((raw, before, backward))
+    raw, backward = lax.optimization_barrier((raw, backward))
+    before, _ = lax.optimization_barrier((before, raw))
     forward = conv(True, (key_feats, value_feats), (queries, grad_out), before, forward_rows)
     raw = jnp.sum(spread_over(raw, ("y",)), axis=0)
     raw, forward = lax.optimization_barrier((raw, forward))

time: 73.5 us -> 69.2 us (0.941)
  starting transfers between devices: 26.2 us -> 21.5 us
    all_to_all x2, starting transfers between devices: 21.5 us -> 15.6 us  [spread_over(): return lax.all_to_all(spread, axes, split_axis=0, concat_axis=0, tiled=True)]
    all_to_all x2, waiting for transfers between devices: 6.38 us -> 9.85 us  [spread_over(): return lax.all_to_all(spread, axes, split_axis=0, concat_axis=0, tiled=True)]
    ppermute x1, waiting for transfers between devices: 1.95 us -> 0.01 us  [shards(): before = lax.ppermute(tail, CTX, [(i, i + 1) for i in range(owners - 1)])]
    ppermute x1, starting transfers between devices: 3.37 us -> 4.59 us  [shards(): before = lax.ppermute(tail, CTX, [(i, i + 1) for i in range(owners - 1)])]
    ppermute x1, waiting for transfers between devices: 0.98 us -> 0.01 us  [shards(): after = lax.ppermute(head, CTX, [(i + 1, i) for i in range(owners - 1)])]
  transfers between devices with their start and end apart: 4 -> 4, of which waited for: 3 -> 2; matrix products, arithmetic and copies ran while one was open for 0% -> 1% of each run, Pallas kernels for 11% -> 14%
where the time goes in v4:
time: 69.2 us; the launch traced here: 68.7 us
  starting transfers between devices  21.5 us (31%)
  blocking collectives  20.2 us (29%)
  Pallas kernels  10.3 us (15%)
  waiting for transfers between devices  9.85 us (14%)
  local copies, waits for them, and re-layouts  4.75 us (7%)
  other arithmetic  1.3 us (2%)
  between operations  0.8 us (1%)
    all_to_all x1, blocking collectives, spread_over(): return lax.all_to_all(spread, axes, split_axis=0, concat_axis=0, tiled=True)  20.2 us
    all_to_all x2, starting transfers between devices, spread_over(): return lax.all_to_all(spread, axes, split_axis=0, concat_axis=0, tiled=True)  15.6 us
    all_to_all x2, waiting for transfers between devices, spread_over(): return lax.all_to_all(spread, axes, split_axis=0, concat_axis=0, tiled=True)  9.85 us
    pallas_call x2, Pallas kernels, conv(): pl.pallas_call(functools.partial(conv_kernel, causal), in_specs=[VMEM] *...  5.6 us
    ppermute x1, starting transfers between devices, shards(): before = lax.ppermute(tail, CTX, [(i, i + 1) for i in range(owners - 1)])  4.59 us
    unnamed x16, local copies, waits for them, and re-layouts  3.15 us
    pallas_call x1, Pallas kernels, local_filter(): pl.pallas_call(local_kernel, in_specs=[VMEM] * 4, out_specs=[VMEM] * 2, o...  2.27 us
    pallas_call x1, Pallas kernels, edge_filter(): pl.pallas_call(edge_kernel, in_specs=[VMEM] * 3, out_specs=VMEM, out_shap...  1.69 us
  transfers between devices with their start and end apart: 4, of which 2 were waited for; matrix products, arithmetic and copies ran while one was open for 1% of the time, Pallas kernels for 14%

profile of v4, /device:TPU:1, one launch (start us, length us, event | category | flops | bytes accessed | tf_op | source)
XLA Modules:
  0.0 68.7 jit_solution(18276588695884690153)
XLA Ops:
  0.6 0.0 copy-start
  0.6 1.2 %multiply_convert_fusion = bf16[128,1024]{1,0:T(8,128)(2,1)S(1)} fusion(bf16[256,1024]{1,0:T(8,128)(2,1)} %x_ref.3, bf16[256,1024]{1,0:T(8,128)(2,1)} %y_ref.3), kind=kLoop, calls=%fused_computation | loop fusion | flops 524288 | bytes 786432 | tf_op jit(solution)/shard_map/convert_element_type | solution.py:27
  1.8 1.3 %collective-permute-start = (bf16[128,1024]{1,0:T(8,128)(2,1)S(1)}, bf16[128,1024]{1,0:T(8,128)(2,1)S(1)}, u32[]{:S(2)}, u32[]{:S(2)}) collective-permute-start(bf16[128,1024]{1,0:T(8,128)(2,1)S(1)} %multiply_convert_fusion), channel_id=1, source_target_pairs={{8,0},{16,8},{24,16},{32,24},{40,32},{48,40},{56,48},{64,56},{72,6... | collective-permute-start | bytes 786440 | tf_op jit(solution)/shard_map/ppermute | solution.py:209
  3.1 0.0 copy-done
  3.1 0.0 copy-start.1
  3.1 1.0 %copy-done.1 = bf16[256,1024]{1,0:T(8,128)(2,1)S(1)} copy-done((bf16[256,1024]{1,0:T(8,128)(2,1)S(1)}, bf16[256,1024]{1,0:T(8,128)(2,1)}, u32[]{:S(2)}) %copy-start.1) | copy-done | bytes 524312
  4.2 0.0 copy-start.3
  4.2 1.0 %copy-done.3 = bf16[256,1024]{1,0:T(8,128)(2,1)S(1)} copy-done((bf16[256,1024]{1,0:T(8,128)(2,1)S(1)}, bf16[256,1024]{1,0:T(8,128)(2,1)}, u32[]{:S(2)}) %copy-start.3) | copy-done | bytes 524312
  5.2 0.0 copy-start.5
  5.2 1.0 %copy-done.5 = bf16[256,1024]{1,0:T(8,128)(2,1)S(1)} copy-done((bf16[256,1024]{1,0:T(8,128)(2,1)S(1)}, bf16[256,1024]{1,0:T(8,128)(2,1)}, u32[]{:S(2)}) %copy-start.5) | copy-done | bytes 524312
  6.2 0.0 copy-start.7
  6.2 2.3 %local_filter.1 = (f32[64,128]{1,0:T(8,128)S(1)}, bf16[128,1024]{1,0:T(8,128)(2,1)S(1)}) custom-call(bf16[256,1024]{1,0:T(8,128)(2,1)S(1)} %copy-done, bf16[256,1024]{1,0:T(8,128)(2,1)S(1)} %copy-done.3, bf16[256,1024]{1,0:T(8,128)(2,1)S(1)} %copy-done.5, bf16[256,1024]{1,0:T(8,128)(2,1)S(1)} %copy-done.1), custom_call_target="tpu_custom_call" | custom-call | flops 3000000000 | bytes 2097152 | tf_op jit(solution)/shard_map/local_filter/pallas_call | solution.py:145
  8.5 4.6 %collective-permute-start.1 = (bf16[128,1024]{1,0:T(8,128)(2,1)S(1)}, bf16[128,1024]{1,0:T(8,128)(2,1)S(1)}, u32[]{:S(2)}, u32[]{:S(2)}) collective-permute-start(bf16[128,1024]{1,0:T(8,128)(2,1)S(1)} %get-tuple-element.20.tail_ref), channel_id=1, source_target_pairs={{0,8},{8,16},{16,24},{24,32},{32,40},{40,48},{48,56},{56,64},{64,7... | collective-permute-start | bytes 786440 | tf_op jit(solution)/shard_map/ppermute | solution.py:218
  13.1 0.0 copy-done.7
  13.1 0.1 rev.3
  13.2 0.1 pad.3.clone
  13.3 0.1 maximum_maximum_fusion.filter_ref
  13.4 0.0 collective-permute-done.after_ref.halo_ref
  13.4 0.0 copy-start.4
  13.4 0.0 copy-start.6
  13.4 1.7 %edge_filter.1 = f32[64,128]{1,0:T(8,128)S(1)} custom-call(bf16[128,1024]{1,0:T(8,128)(2,1)S(1)} %get-tuple-element.20.tail_ref, bf16[128,1024]{1,0:T(8,128)(2,1)S(1)} %collective-permute-done.after_ref.halo_ref, f32[64,128]{1,0:T(8,128)S(1)} %get-tuple-element.21.local_ref), custom_call_target="tpu_custom_call" | custom-call | flops 1000000000 | bytes 524288 | tf_op jit(solution)/shard_map/edge_filter/pallas_call | solution.py:161
  15.1 0.0 copy-start.2
  15.1 0.7 %broadcast_in_dim.6 = f32[8,64,128]{2,1,0:T(8,128)} broadcast(f32[64,128]{1,0:T(8,128)S(1)} %edge_filter.1), dimensions={1,2} | broadcast | bytes 294912 | tf_op jit(solution)/shard_map/broadcast_in_dim | solution.py:201
  15.9 8.8 %all-to-all-start = ((f32[8,64,128]{2,1,0:T(8,128)}), f32[8,64,128]{2,1,0:T(8,128)S(1)}, u32[]{:S(2)}, u32[]{:S(2)}) async-start(f32[8,64,128]{2,1,0:T(8,128)} %broadcast_in_dim.6), calls=%async_computation | async-start | bytes 524288 | tf_op jit(solution)/shard_map/all_to_all | solution.py:202
  24.6 0.0 collective-permute-done.1.halo_ref
  24.6 0.0 copy-done.4
  24.6 0.0 copy-done.6
  24.7 0.0 copy-done.2
  24.7 2.8 %backward_conv.1 = (bf16[256,1024]{1,0:T(8,128)(2,1)}, bf16[256,1024]{1,0:T(8,128)(2,1)}) custom-call(bf16[256,1024]{1,0:T(8,128)(2,1)S(1)} %copy-done.2, bf16[256,1024]{1,0:T(8,128)(2,1)S(1)} %copy-done, bf16[256,1024]{1,0:T(8,128)(2,1)S(1)} %copy-done.6, bf16[256,1024]{1,0:T(8,128)(2,1)S(1)} %copy-done.4, ...), custom_call_target="tpu_custom_call" | custom-call | flops 10000000000 | bytes 3145728 | tf_op jit(solution)/shard_map/backward_conv/pallas_call | solution.py:175
  27.5 3.2 %all-to-all-done = f32[8,64,128]{2,1,0:T(8,128)S(1)} async-done(((f32[8,64,128]{2,1,0:T(8,128)}), f32[8,64,128]{2,1,0:T(8,128)S(1)}, u32[]{:S(2)}, u32[]{:S(2)}) %all-to-all-start) | async-done | bytes 262176 | tf_op jit(solution)/shard_map/all_to_all | solution.py:202
  30.8 0.7 %broadcast_in_dim.7 = f32[8,64,128]{2,1,0:T(8,128)} broadcast(f32[64,128]{1,0:T(8,128)S(1)} %reduce_sum.27), dimensions={1,2} | broadcast | bytes 294912 | tf_op jit(solution)/shard_map/broadcast_in_dim | solution.py:201
  31.5 6.8 %all-to-all-start.1 = ((f32[8,64,128]{2,1,0:T(8,128)}), f32[8,64,128]{2,1,0:T(8,128)S(1)}, u32[]{:S(2)}, u32[]{:S(2)}) async-start(f32[8,64,128]{2,1,0:T(8,128)} %broadcast_in_dim.7), calls=%async_computation.1 | async-start | bytes 524288 | tf_op jit(solution)/shard_map/all_to_all | solution.py:202
  38.3 2.8 %forward_conv.1 = (bf16[256,1024]{1,0:T(8,128)(2,1)}, bf16[256,1024]{1,0:T(8,128)(2,1)}) custom-call(bf16[256,1024]{1,0:T(8,128)(2,1)S(1)} %copy-done.4, bf16[256,1024]{1,0:T(8,128)(2,1)S(1)} %copy-done.6, bf16[256,1024]{1,0:T(8,128)(2,1)S(1)} %copy-done, bf16[256,1024]{1,0:T(8,128)(2,1)S(1)} %copy-done.2, ...), custom_call_target="tpu_custom_call" | custom-call | flops 10000000000 | bytes 3145728 | tf_op jit(solution)/shard_map/forward_conv/pallas_call | solution.py:175
  41.1 6.6 %all-to-all-done.1 = f32[8,64,128]{2,1,0:T(8,128)S(1)} async-done(((f32[8,64,128]{2,1,0:T(8,128)}), f32[8,64,128]{2,1,0:T(8,128)S(1)}, u32[]{:S(2)}, u32[]{:S(2)}) %all-to-all-start.1) | async-done | bytes 262176 | tf_op jit(solution)/shard_map/all_to_all | solution.py:202
  47.8 20.2 %all_to_all.15.squares_ref = f32[8,1,128]{2,1,0:T(1,128)S(1)} all-to-all(f32[8,1,128]{2,1,0:T(1,128)S(1)} %broadcast_in_dim.8), channel_id=1, replica_groups=mesh['y'=8,'zl'=2,'x'=4,'zh'=4,'core'=2] {'zh','core'}, dimensions={0} | all-to-all | bytes 8192 | tf_op jit(solution)/shard_map/all_to_all | solution.py:202
  68.0 0.7 %scale.1 = f32[64,128]{1,0:T(8,128)} custom-call(f32[64,128]{1,0:T(8,128)S(1)} %reduce_sum.28.raw_ref, f32[8,1,128]{2,1,0:T(1,128)S(1)} %all_to_all.15.squares_ref), custom_call_target="tpu_custom_call" | custom-call | tf_op jit(solution)/shard_map/scale/pallas_call | solution.py:189
  (7 shorter events, 0.1 us)
Async XLA Ops:
  0.6 2.5 %copy-start = (bf16[256,1024]{1,0:T(8,128)(2,1)S(1)}, bf16[256,1024]{1,0:T(8,128)(2,1)}, u32[]{:S(2)}) copy-start(bf16[256,1024]{1,0:T(8,128)(2,1)} %x_ref.3) | copy-start | bytes 1572868
  1.8 11.6 %collective-permute-start = (bf16[128,1024]{1,0:T(8,128)(2,1)S(1)}, bf16[128,1024]{1,0:T(8,128)(2,1)S(1)}, u32[]{:S(2)}, u32[]{:S(2)}) collective-permute-start(bf16[128,1024]{1,0:T(8,128)(2,1)S(1)} %multiply_convert_fusion), channel_id=1, source_target_pairs={{8,0},{16,8},{24,16},{32,24},{40,32},{48,40},{56,48},{64,56},{72,6... | collective-permute-start | bytes 786440 | tf_op jit(solution)/shard_map/ppermute | solution.py:209
  3.1 1.0 %copy-start.1 = (bf16[256,1024]{1,0:T(8,128)(2,1)S(1)}, bf16[256,1024]{1,0:T(8,128)(2,1)}, u32[]{:S(2)}) copy-start(bf16[256,1024]{1,0:T(8,128)(2,1)} %y_ref.3) | copy-start | bytes 1572868
  4.2 1.0 %copy-start.3 = (bf16[256,1024]{1,0:T(8,128)(2,1)S(1)}, bf16[256,1024]{1,0:T(8,128)(2,1)}, u32[]{:S(2)}) copy-start(bf16[256,1024]{1,0:T(8,128)(2,1)} %a_ref.3) | copy-start | bytes 1572868
  5.2 1.0 %copy-start.5 = (bf16[256,1024]{1,0:T(8,128)(2,1)S(1)}, bf16[256,1024]{1,0:T(8,128)(2,1)}, u32[]{:S(2)}) copy-start(bf16[256,1024]{1,0:T(8,128)(2,1)} %b_ref.3) | copy-start | bytes 1572868
  6.2 6.9 %copy-start.7 = (bf16[64,128]{1,0:T(8,128)(2,1)S(1)}, bf16[64,128]{1,0:T(8,128)(2,1)}, u32[]{:S(2)}) copy-start(bf16[64,128]{1,0:T(8,128)(2,1)} %param.8) | copy-start | bytes 49156
  8.5 16.1 %collective-permute-start.1 = (bf16[128,1024]{1,0:T(8,128)(2,1)S(1)}, bf16[128,1024]{1,0:T(8,128)(2,1)S(1)}, u32[]{:S(2)}, u32[]{:S(2)}) collective-permute-start(bf16[128,1024]{1,0:T(8,128)(2,1)S(1)} %get-tuple-element.20.tail_ref), channel_id=1, source_target_pairs={{0,8},{8,16},{16,24},{24,32},{32,40},{40,48},{48,56},{56,64},{64,7... | collective-permute-start | bytes 786440 | tf_op jit(solution)/shard_map/ppermute | solution.py:218
  13.4 11.2 %copy-start.4 = (bf16[256,1024]{1,0:T(8,128)(2,1)S(1)}, bf16[256,1024]{1,0:T(8,128)(2,1)}, u32[]{:S(2)}) copy-start(bf16[256,1024]{1,0:T(8,128)(2,1)} %a_ref.3) | copy-start | bytes 1572868
  13.4 11.2 %copy-start.6 = (bf16[256,1024]{1,0:T(8,128)(2,1)S(1)}, bf16[256,1024]{1,0:T(8,128)(2,1)}, u32[]{:S(2)}) copy-start(bf16[256,1024]{1,0:T(8,128)(2,1)} %b_ref.3) | copy-start | bytes 1572868
  15.1 9.5 %copy-start.2 = (bf16[256,1024]{1,0:T(8,128)(2,1)S(1)}, bf16[256,1024]{1,0:T(8,128)(2,1)}, u32[]{:S(2)}) copy-start(bf16[256,1024]{1,0:T(8,128)(2,1)} %y_ref.3) | copy-start | bytes 1572868
  15.9 14.9 %all-to-all-start = ((f32[8,64,128]{2,1,0:T(8,128)}), f32[8,64,128]{2,1,0:T(8,128)S(1)}, u32[]{:S(2)}, u32[]{:S(2)}) async-start(f32[8,64,128]{2,1,0:T(8,128)} %broadcast_in_dim.6), calls=%async_computation | async-start | bytes 524288 | tf_op jit(solution)/shard_map/all_to_all | solution.py:202
  31.5 16.2 %all-to-all-start.1 = ((f32[8,64,128]{2,1,0:T(8,128)}), f32[8,64,128]{2,1,0:T(8,128)S(1)}, u32[]{:S(2)}, u32[]{:S(2)}) async-start(f32[8,64,128]{2,1,0:T(8,128)} %broadcast_in_dim.7), calls=%async_computation.1 | async-start | bytes 524288 | tf_op jit(solution)/shard_map/all_to_all | solution.py:202

commit v5 on v4

--- a/solution.py
+++ b/solution.py
@@ -16,6 +16,7 @@
 LANES = 128
 UNROLL = 4
 LIMIT = 8 << 20
+LOCAL_LIMIT = 107 << 19
 TILE_GROUPS = LANES // G
 CTX = ("y", "zl", "x")
 MP = ("zh", "core")
@@ -66,15 +67,30 @@
     return pl.ds(pl.multiple_of(tile * LANES, LANES), LANES)
 
 
-def local_kernel(q_ref, k_ref, v_ref, go_ref, raw_ref, tail_ref, rows):
-    tokens = q_ref.shape[0]
-
-    @pl.loop(0, q_ref.shape[1] // LANES, unroll=UNROLL)
-    def _(t):
-        c = lanes_of(t)
-        product = product_of(k_ref[:, c], v_ref[:, c])
-        tail_ref[:, c] = product[tokens - K :]
-        correlate(product, product_of(go_ref[:, c], q_ref[:, c]), t, rows)
+def local_kernel(q_hbm, k_hbm, v_hbm, go_hbm, raw_ref, tail_ref, q_buf, k_buf, v_buf, go_buf, rows, sems):
+    tokens, channels = q_buf.shape
+    chunk = UNROLL * LANES
+
+    def copies_of(i):
+        c = pl.ds(pl.multiple_of(i * chunk, chunk), chunk)
+        pairs = ((k_hbm, k_buf), (v_hbm, v_buf), (go_hbm, go_buf), (q_hbm, q_buf))
+        return [pltpu.make_async_copy(src.at[:, c], dst.at[:, c], sems.at[n, i]) for n, (src, dst) in enumerate(pairs)]
+
+    @pl.loop(0, channels // chunk)
+    def _(i):
+        for copy in copies_of(i):
+            copy.start()
+
+    @pl.loop(0, channels // chunk)
+    def _(i):
+        for copy in copies_of(i):
+            copy.wait()
+        for u in range(UNROLL):
+            t = i * UNROLL + u
+            c = lanes_of(t)
+            product = product_of(k_buf[:, c], v_buf[:, c])
+            tail_ref[:, c] = product[tokens - K :]
+            correlate(product, product_of(go_buf[:, c], q_buf[:, c]), t, rows)
 
     raw_ref[...] = fold(rows)
 
@@ -144,15 +160,19 @@
 def local_filter(q, k, v, go, slab_groups):
     return pl.pallas_call(
         local_kernel,
-        in_specs=[VMEM] * 4,
+        in_specs=[HBM] * 4,
         out_specs=[VMEM] * 2,
         out_shape=[
             jax.ShapeDtypeStruct((slab_groups, K), jnp.float32),
             jax.ShapeDtypeStruct((K, q.shape[1]), jnp.bfloat16),
         ],
-        scratch_shapes=[pltpu.VMEM((slab_groups * 8, W), jnp.float32)],
+        scratch_shapes=[pltpu.VMEM(q.shape, jnp.bfloat16)] * 4
+        + [
+            pltpu.VMEM((slab_groups * 8, W), jnp.float32),
+            pltpu.SemaphoreType.DMA((4, q.shape[1] // (UNROLL * LANES))),
+        ],
         cost_estimate=pl.CostEstimate(flops=3 * 10**9, bytes_accessed=2**21, transcendentals=0),
-        compiler_params=pltpu.CompilerParams(vmem_limit_bytes=LIMIT),
+        compiler_params=pltpu.CompilerParams(vmem_limit_bytes=LOCAL_LIMIT),
         name="local_filter",
     )(q, k, v, go)
 

time: 69.2 us -> 67.4 us (0.974)
  local copies, waits for them, and re-layouts: 4.75 us -> 1.64 us
  Pallas kernels: 10.3 us -> 11.6 us
    unnamed x16 -> x10, local copies, waits for them, and re-layouts: 3.15 us -> 0.03 us
    pallas_call x1, Pallas kernels: 2.27 us -> 3.55 us  [local_filter(): pl.pallas_call(local_kernel, in_specs=[HBM] * 4, out_specs=[VMEM] * 2, ou...]
  transfers between devices with their start and end apart: 4 -> 4, of which waited for: 2 -> 2; matrix products, arithmetic and copies ran while one was open for 1% -> 1% of each run, Pallas kernels for 14% -> 16%
where the time goes in v5:
time: 67.4 us; the launch traced here: 67 us
  starting transfers between devices  21.5 us (32%)
  blocking collectives  20.4 us (30%)
  Pallas kernels  11.6 us (17%)
  waiting for transfers between devices  9.87 us (15%)
  local copies, waits for them, and re-layouts  1.64 us (2%)
  other arithmetic  1.24 us (2%)
  between operations  0.8 us (1%)
    all_to_all x1, blocking collectives, spread_over(): return lax.all_to_all(spread, axes, split_axis=0, concat_axis=0, tiled=True)  20.4 us
    all_to_all x2, starting transfers between devices, spread_over(): return lax.all_to_all(spread, axes, split_axis=0, concat_axis=0, tiled=True)  15.6 us
    all_to_all x2, waiting for transfers between devices, spread_over(): return lax.all_to_all(spread, axes, split_axis=0, concat_axis=0, tiled=True)  9.87 us
    pallas_call x2, Pallas kernels, conv(): pl.pallas_call(functools.partial(conv_kernel, causal), in_specs=[VMEM] *...  5.6 us
    ppermute x1, starting transfers between devices, shards(): before = lax.ppermute(tail, CTX, [(i, i + 1) for i in range(owners - 1)])  4.59 us
    pallas_call x1, Pallas kernels, local_filter(): pl.pallas_call(local_kernel, in_specs=[HBM] * 4, out_specs=[VMEM] * 2, ou...  3.55 us
    pallas_call x1, Pallas kernels, edge_filter(): pl.pallas_call(edge_kernel, in_specs=[VMEM] * 3, out_specs=VMEM, out_shap...  1.68 us
    broadcast_in_dim x3, local copies, waits for them, and re-layouts, spread_over(): spread = jnp.broadcast_to(value[None], (size,) + value.shape)  1.44 us
  transfers between devices with their start and end apart: 4, of which 2 were waited for; matrix products, arithmetic and copies ran while one was open for 1% of the time, Pallas kernels for 16%

profile of v5, /device:TPU:1, one launch (start us, length us, event | category | flops | bytes accessed | tf_op | source)
XLA Modules:
  0.0 67.0 jit_solution(3854727071636143385)
XLA Ops:
  0.6 1.1 %multiply_convert_fusion = bf16[128,1024]{1,0:T(8,128)(2,1)S(1)} fusion(bf16[256,1024]{1,0:T(8,128)(2,1)} %x_ref.3, bf16[256,1024]{1,0:T(8,128)(2,1)} %y_ref.3), kind=kLoop, calls=%fused_computation | loop fusion | flops 524288 | bytes 786432 | tf_op jit(solution)/shard_map/convert_element_type | solution.py:28
  1.7 0.0 copy-start.4
  1.7 1.3 %collective-permute-start = (bf16[128,1024]{1,0:T(8,128)(2,1)S(1)}, bf16[128,1024]{1,0:T(8,128)(2,1)S(1)}, u32[]{:S(2)}, u32[]{:S(2)}) collective-permute-start(bf16[128,1024]{1,0:T(8,128)(2,1)S(1)} %multiply_convert_fusion), channel_id=1, source_target_pairs={{8,0},{16,8},{24,16},{32,24},{40,32},{48,40},{56,48},{64,56},{72,6... | collective-permute-start | bytes 786440 | tf_op jit(solution)/shard_map/ppermute | solution.py:229
  3.0 3.6 %local_filter.1 = (f32[64,128]{1,0:T(8,128)S(1)}, bf16[128,1024]{1,0:T(8,128)(2,1)S(1)}) custom-call(bf16[256,1024]{1,0:T(8,128)(2,1)} %x_ref.3, bf16[256,1024]{1,0:T(8,128)(2,1)} %a_ref.3, bf16[256,1024]{1,0:T(8,128)(2,1)} %b_ref.3, bf16[256,1024]{1,0:T(8,128)(2,1)} %y_ref.3), custom_call_target="tpu_custom_call" | custom-call | flops 3000000000 | bytes 2097152 | tf_op jit(solution)/shard_map/local_filter/pallas_call | solution.py:161
  6.6 4.6 %collective-permute-start.1 = (bf16[128,1024]{1,0:T(8,128)(2,1)S(1)}, bf16[128,1024]{1,0:T(8,128)(2,1)S(1)}, u32[]{:S(2)}, u32[]{:S(2)}) collective-permute-start(bf16[128,1024]{1,0:T(8,128)(2,1)S(1)} %get-tuple-element.20.tail_ref), channel_id=1, source_target_pairs={{0,8},{8,16},{16,24},{24,32},{32,40},{40,48},{48,56},{56,64},{64,7... | collective-permute-start | bytes 786440 | tf_op jit(solution)/shard_map/ppermute | solution.py:238
  11.2 0.0 copy-done.4
  11.2 0.1 rev.3
  11.3 0.1 pad.3.clone
  11.4 0.1 maximum_maximum_fusion.filter_ref
  11.5 0.0 collective-permute-done.after_ref.halo_ref
  11.5 0.0 copy-start.1
  11.5 0.0 copy-start.2
  11.5 0.0 copy-start.3
  11.5 1.7 %edge_filter.1 = f32[64,128]{1,0:T(8,128)S(1)} custom-call(bf16[128,1024]{1,0:T(8,128)(2,1)S(1)} %get-tuple-element.20.tail_ref, bf16[128,1024]{1,0:T(8,128)(2,1)S(1)} %collective-permute-done.after_ref.halo_ref, f32[64,128]{1,0:T(8,128)S(1)} %get-tuple-element.21.local_ref), custom_call_target="tpu_custom_call" | custom-call | flops 1000000000 | bytes 524288 | tf_op jit(solution)/shard_map/edge_filter/pallas_call | solution.py:181
  13.2 0.0 copy-start
  13.2 0.7 %broadcast_in_dim.6 = f32[8,64,128]{2,1,0:T(8,128)} broadcast(f32[64,128]{1,0:T(8,128)S(1)} %edge_filter.1), dimensions={1,2} | broadcast | bytes 294912 | tf_op jit(solution)/shard_map/broadcast_in_dim | solution.py:221
  13.9 8.8 %all-to-all-start = ((f32[8,64,128]{2,1,0:T(8,128)}), f32[8,64,128]{2,1,0:T(8,128)S(1)}, u32[]{:S(2)}, u32[]{:S(2)}) async-start(f32[8,64,128]{2,1,0:T(8,128)} %broadcast_in_dim.6), calls=%async_computation | async-start | bytes 524288 | tf_op jit(solution)/shard_map/all_to_all | solution.py:222
  22.8 0.0 collective-permute-done.1.halo_ref
  22.8 0.0 copy-done.1
  22.8 0.0 copy-done.2
  22.8 0.0 copy-done.3
  22.8 0.0 copy-done
  22.8 2.8 %backward_conv.1 = (bf16[256,1024]{1,0:T(8,128)(2,1)}, bf16[256,1024]{1,0:T(8,128)(2,1)}) custom-call(bf16[256,1024]{1,0:T(8,128)(2,1)S(1)} %copy-done.1, bf16[256,1024]{1,0:T(8,128)(2,1)S(1)} %copy-done, bf16[256,1024]{1,0:T(8,128)(2,1)S(1)} %copy-done.3, bf16[256,1024]{1,0:T(8,128)(2,1)S(1)} %copy-done.2, ...), custom_call_target="tpu_custom_call" | custom-call | flops 10000000000 | bytes 3145728 | tf_op jit(solution)/shard_map/backward_conv/pallas_call | solution.py:195
  25.6 3.2 %all-to-all-done = f32[8,64,128]{2,1,0:T(8,128)S(1)} async-done(((f32[8,64,128]{2,1,0:T(8,128)}), f32[8,64,128]{2,1,0:T(8,128)S(1)}, u32[]{:S(2)}, u32[]{:S(2)}) %all-to-all-start) | async-done | bytes 262176 | tf_op jit(solution)/shard_map/all_to_all | solution.py:222
  28.9 0.7 %broadcast_in_dim.7 = f32[8,64,128]{2,1,0:T(8,128)} broadcast(f32[64,128]{1,0:T(8,128)S(1)} %reduce_sum.27), dimensions={1,2} | broadcast | bytes 294912 | tf_op jit(solution)/shard_map/broadcast_in_dim | solution.py:221
  29.6 6.8 %all-to-all-start.1 = ((f32[8,64,128]{2,1,0:T(8,128)}), f32[8,64,128]{2,1,0:T(8,128)S(1)}, u32[]{:S(2)}, u32[]{:S(2)}) async-start(f32[8,64,128]{2,1,0:T(8,128)} %broadcast_in_dim.7), calls=%async_computation.1 | async-start | bytes 524288 | tf_op jit(solution)/shard_map/all_to_all | solution.py:222
  36.4 2.8 %forward_conv.1 = (bf16[256,1024]{1,0:T(8,128)(2,1)}, bf16[256,1024]{1,0:T(8,128)(2,1)}) custom-call(bf16[256,1024]{1,0:T(8,128)(2,1)S(1)} %copy-done.2, bf16[256,1024]{1,0:T(8,128)(2,1)S(1)} %copy-done.3, bf16[256,1024]{1,0:T(8,128)(2,1)S(1)} %copy-done, bf16[256,1024]{1,0:T(8,128)(2,1)S(1)} %copy-done.1, ...), custom_call_target="tpu_custom_call" | custom-call | flops 10000000000 | bytes 3145728 | tf_op jit(solution)/shard_map/forward_conv/pallas_call | solution.py:195
  39.2 6.6 %all-to-all-done.1 = f32[8,64,128]{2,1,0:T(8,128)S(1)} async-done(((f32[8,64,128]{2,1,0:T(8,128)}), f32[8,64,128]{2,1,0:T(8,128)S(1)}, u32[]{:S(2)}, u32[]{:S(2)}) %all-to-all-start.1) | async-done | bytes 262176 | tf_op jit(solution)/shard_map/all_to_all | solution.py:222
  45.9 20.4 %all_to_all.15.squares_ref = f32[8,1,128]{2,1,0:T(1,128)S(1)} all-to-all(f32[8,1,128]{2,1,0:T(1,128)S(1)} %broadcast_in_dim.8), channel_id=1, replica_groups=mesh['y'=8,'zl'=2,'x'=4,'zh'=4,'core'=2] {'zh','core'}, dimensions={0} | all-to-all | bytes 8192 | tf_op jit(solution)/shard_map/all_to_all | solution.py:222
  66.3 0.7 %scale.1 = f32[64,128]{1,0:T(8,128)} custom-call(f32[64,128]{1,0:T(8,128)S(1)} %reduce_sum.28.raw_ref, f32[8,1,128]{2,1,0:T(1,128)S(1)} %all_to_all.15.squares_ref), custom_call_target="tpu_custom_call" | custom-call | tf_op jit(solution)/shard_map/scale/pallas_call | solution.py:209
  (7 shorter events, 0.1 us)
Async XLA Ops:
  1.7 9.5 %copy-start.4 = (bf16[64,128]{1,0:T(8,128)(2,1)S(1)}, bf16[64,128]{1,0:T(8,128)(2,1)}, u32[]{:S(2)}) copy-start(bf16[64,128]{1,0:T(8,128)(2,1)} %param.8) | copy-start | bytes 49156
  1.7 9.7 %collective-permute-start = (bf16[128,1024]{1,0:T(8,128)(2,1)S(1)}, bf16[128,1024]{1,0:T(8,128)(2,1)S(1)}, u32[]{:S(2)}, u32[]{:S(2)}) collective-permute-start(bf16[128,1024]{1,0:T(8,128)(2,1)S(1)} %multiply_convert_fusion), channel_id=1, source_target_pairs={{8,0},{16,8},{24,16},{32,24},{40,32},{48,40},{56,48},{64,56},{72,6... | collective-permute-start | bytes 786440 | tf_op jit(solution)/shard_map/ppermute | solution.py:229
  6.6 16.2 %collective-permute-start.1 = (bf16[128,1024]{1,0:T(8,128)(2,1)S(1)}, bf16[128,1024]{1,0:T(8,128)(2,1)S(1)}, u32[]{:S(2)}, u32[]{:S(2)}) collective-permute-start(bf16[128,1024]{1,0:T(8,128)(2,1)S(1)} %get-tuple-element.20.tail_ref), channel_id=1, source_target_pairs={{0,8},{8,16},{16,24},{24,32},{32,40},{40,48},{48,56},{56,64},{64,7... | collective-permute-start | bytes 786440 | tf_op jit(solution)/shard_map/ppermute | solution.py:238
  11.5 11.3 %copy-start.1 = (bf16[256,1024]{1,0:T(8,128)(2,1)S(1)}, bf16[256,1024]{1,0:T(8,128)(2,1)}, u32[]{:S(2)}) copy-start(bf16[256,1024]{1,0:T(8,128)(2,1)} %y_ref.3) | copy-start | bytes 1572868
  11.5 11.3 %copy-start.2 = (bf16[256,1024]{1,0:T(8,128)(2,1)S(1)}, bf16[256,1024]{1,0:T(8,128)(2,1)}, u32[]{:S(2)}) copy-start(bf16[256,1024]{1,0:T(8,128)(2,1)} %a_ref.3) | copy-start | bytes 1572868
  11.5 11.3 %copy-start.3 = (bf16[256,1024]{1,0:T(8,128)(2,1)S(1)}, bf16[256,1024]{1,0:T(8,128)(2,1)}, u32[]{:S(2)}) copy-start(bf16[256,1024]{1,0:T(8,128)(2,1)} %b_ref.3) | copy-start | bytes 1572868
  13.2 9.6 %copy-start = (bf16[256,1024]{1,0:T(8,128)(2,1)S(1)}, bf16[256,1024]{1,0:T(8,128)(2,1)}, u32[]{:S(2)}) copy-start(bf16[256,1024]{1,0:T(8,128)(2,1)} %x_ref.3) | copy-start | bytes 1572868
  13.9 14.9 %all-to-all-start = ((f32[8,64,128]{2,1,0:T(8,128)}), f32[8,64,128]{2,1,0:T(8,128)S(1)}, u32[]{:S(2)}, u32[]{:S(2)}) async-start(f32[8,64,128]{2,1,0:T(8,128)} %broadcast_in_dim.6), calls=%async_computation | async-start | bytes 524288 | tf_op jit(solution)/shard_map/all_to_all | solution.py:222
  29.6 16.3 %all-to-all-start.1 = ((f32[8,64,128]{2,1,0:T(8,128)}), f32[8,64,128]{2,1,0:T(8,128)S(1)}, u32[]{:S(2)}, u32[]{:S(2)}) async-start(f32[8,64,128]{2,1,0:T(8,128)} %broadcast_in_dim.7), calls=%async_computation.1 | async-start | bytes 524288 | tf_op jit(solution)/shard_map/all_to_all | solution.py:222

commit v6 on v5

--- a/solution.py
+++ b/solution.py
@@ -216,10 +216,19 @@
     )(raw, squares)
 
 
-def spread_over(value, axes):
-    size = lax.axis_size(axes)
+def spread_over(value, axes, groups=None):
+    size = len(groups[0]) if groups else lax.axis_size(axes)
     spread = jnp.broadcast_to(value[None], (size,) + value.shape)
-    return lax.all_to_all(spread, axes, split_axis=0, concat_axis=0, tiled=True)
+    return lax.all_to_all(spread, axes, split_axis=0, concat_axis=0, tiled=True, axis_index_groups=groups)
+
+
+def slab_groups_along_z():
+    highs, cores = lax.axis_size("zh"), lax.axis_size("core")
+
+    def index(z, core):
+        return ((z % 2) * highs + z // 2) * cores + core
+
+    return [[index(z, core) for z in chips for core in range(cores)] for chips in ((1, 2, 4, 7), (0, 3, 5, 6))]
 
 
 def shards(queries, key_feats, value_feats, filters, grad_out):
@@ -244,7 +253,7 @@
     forward = conv(True, (key_feats, value_feats), (queries, grad_out), before, forward_rows)
     raw = jnp.sum(spread_over(raw, ("y",)), axis=0)
     raw, forward = lax.optimization_barrier((raw, forward))
-    grad_filters = scale(raw, spread_over(jnp.sum(raw * raw, axis=0, keepdims=True), MP))
+    grad_filters = scale(raw, spread_over(jnp.sum(raw * raw, axis=0, keepdims=True), ("zl",) + MP, slab_groups_along_z()))
     return (*forward, *backward, grad_filters)
 
 

time: 67.4 us -> 66.5 us (0.987)
  blocking collectives: 20.4 us -> 19.5 us
    all_to_all x1, blocking collectives: 20.4 us -> 19.5 us  [spread_over(): lax.all_to_all(spread, axes, split_axis=0, concat_axis=0, tiled=True, axi...]
where the time goes in v6:
time: 66.5 us; the launch traced here: 66.1 us
  starting transfers between devices  21.5 us (32%)
  blocking collectives  19.5 us (29%)
  Pallas kernels  11.6 us (17%)
  waiting for transfers between devices  9.87 us (15%)
  local copies, waits for them, and re-layouts  1.64 us (2%)
  other arithmetic  1.24 us (2%)
  between operations  0.8 us (1%)
    all_to_all x1, blocking collectives, spread_over(): lax.all_to_all(spread, axes, split_axis=0, concat_axis=0, tiled=True, axi...  19.5 us
    all_to_all x2, starting transfers between devices, spread_over(): lax.all_to_all(spread, axes, split_axis=0, concat_axis=0, tiled=True, axi...  15.6 us
    all_to_all x2, waiting for transfers between devices, spread_over(): lax.all_to_all(spread, axes, split_axis=0, concat_axis=0, tiled=True, axi...  9.87 us
    pallas_call x2, Pallas kernels, conv(): pl.pallas_call(functools.partial(conv_kernel, causal), in_specs=[VMEM] *...  5.6 us
    ppermute x1, starting transfers between devices, shards(): before = lax.ppermute(tail, CTX, [(i, i + 1) for i in range(owners - 1)])  4.59 us
    pallas_call x1, Pallas kernels, local_filter(): pl.pallas_call(local_kernel, in_specs=[HBM] * 4, out_specs=[VMEM] * 2, ou...  3.55 us
    pallas_call x1, Pallas kernels, edge_filter(): pl.pallas_call(edge_kernel, in_specs=[VMEM] * 3, out_specs=VMEM, out_shap...  1.68 us
    broadcast_in_dim x3, local copies, waits for them, and re-layouts, spread_over(): spread = jnp.broadcast_to(value[None], (size,) + value.shape)  1.44 us
  transfers between devices with their start and end apart: 4, of which 2 were waited for; matrix products, arithmetic and copies ran while one was open for 1% of the time, Pallas kernels for 16%

profile of v6, /device:TPU:1, one launch (start us, length us, event | category | flops | bytes accessed | tf_op | source)
XLA Modules:
  0.0 66.1 jit_solution(7993547622651546941)
XLA Ops:
  0.6 1.1 %multiply_convert_fusion = bf16[128,1024]{1,0:T(8,128)(2,1)S(1)} fusion(bf16[256,1024]{1,0:T(8,128)(2,1)} %x_ref.3, bf16[256,1024]{1,0:T(8,128)(2,1)} %y_ref.3), kind=kLoop, calls=%fused_computation | loop fusion | flops 524288 | bytes 786432 | tf_op jit(solution)/shard_map/convert_element_type | solution.py:28
  1.7 0.0 copy-start.4
  1.7 1.3 %collective-permute-start = (bf16[128,1024]{1,0:T(8,128)(2,1)S(1)}, bf16[128,1024]{1,0:T(8,128)(2,1)S(1)}, u32[]{:S(2)}, u32[]{:S(2)}) collective-permute-start(bf16[128,1024]{1,0:T(8,128)(2,1)S(1)} %multiply_convert_fusion), channel_id=1, source_target_pairs={{8,0},{16,8},{24,16},{32,24},{40,32},{48,40},{56,48},{64,56},{72,6... | collective-permute-start | bytes 786440 | tf_op jit(solution)/shard_map/ppermute | solution.py:238
  3.0 3.6 %local_filter.1 = (f32[64,128]{1,0:T(8,128)S(1)}, bf16[128,1024]{1,0:T(8,128)(2,1)S(1)}) custom-call(bf16[256,1024]{1,0:T(8,128)(2,1)} %x_ref.3, bf16[256,1024]{1,0:T(8,128)(2,1)} %a_ref.3, bf16[256,1024]{1,0:T(8,128)(2,1)} %b_ref.3, bf16[256,1024]{1,0:T(8,128)(2,1)} %y_ref.3), custom_call_target="tpu_custom_call" | custom-call | flops 3000000000 | bytes 2097152 | tf_op jit(solution)/shard_map/local_filter/pallas_call | solution.py:161
  6.6 4.6 %collective-permute-start.1 = (bf16[128,1024]{1,0:T(8,128)(2,1)S(1)}, bf16[128,1024]{1,0:T(8,128)(2,1)S(1)}, u32[]{:S(2)}, u32[]{:S(2)}) collective-permute-start(bf16[128,1024]{1,0:T(8,128)(2,1)S(1)} %get-tuple-element.20.tail_ref), channel_id=1, source_target_pairs={{0,8},{8,16},{16,24},{24,32},{32,40},{40,48},{48,56},{56,64},{64,7... | collective-permute-start | bytes 786440 | tf_op jit(solution)/shard_map/ppermute | solution.py:247
  11.2 0.0 copy-done.4
  11.2 0.1 rev.3
  11.3 0.1 pad.3.clone
  11.4 0.1 maximum_maximum_fusion.filter_ref
  11.5 0.0 collective-permute-done.after_ref.halo_ref
  11.5 0.0 copy-start.1
  11.5 0.0 copy-start.2
  11.5 0.0 copy-start.3
  11.5 1.7 %edge_filter.1 = f32[64,128]{1,0:T(8,128)S(1)} custom-call(bf16[128,1024]{1,0:T(8,128)(2,1)S(1)} %get-tuple-element.20.tail_ref, bf16[128,1024]{1,0:T(8,128)(2,1)S(1)} %collective-permute-done.after_ref.halo_ref, f32[64,128]{1,0:T(8,128)S(1)} %get-tuple-element.21.local_ref), custom_call_target="tpu_custom_call" | custom-call | flops 1000000000 | bytes 524288 | tf_op jit(solution)/shard_map/edge_filter/pallas_call | solution.py:181
  13.2 0.0 copy-start
  13.2 0.7 %broadcast_in_dim.6 = f32[8,64,128]{2,1,0:T(8,128)} broadcast(f32[64,128]{1,0:T(8,128)S(1)} %edge_filter.1), dimensions={1,2} | broadcast | bytes 294912 | tf_op jit(solution)/shard_map/broadcast_in_dim | solution.py:221
  13.9 8.8 %all-to-all-start = ((f32[8,64,128]{2,1,0:T(8,128)}), f32[8,64,128]{2,1,0:T(8,128)S(1)}, u32[]{:S(2)}, u32[]{:S(2)}) async-start(f32[8,64,128]{2,1,0:T(8,128)} %broadcast_in_dim.6), calls=%async_computation | async-start | bytes 524288 | tf_op jit(solution)/shard_map/all_to_all | solution.py:222
  22.8 0.0 collective-permute-done.1.halo_ref
  22.8 0.0 copy-done.1
  22.8 0.0 copy-done.2
  22.8 0.0 copy-done.3
  22.8 0.0 copy-done
  22.8 2.8 %backward_conv.1 = (bf16[256,1024]{1,0:T(8,128)(2,1)}, bf16[256,1024]{1,0:T(8,128)(2,1)}) custom-call(bf16[256,1024]{1,0:T(8,128)(2,1)S(1)} %copy-done.1, bf16[256,1024]{1,0:T(8,128)(2,1)S(1)} %copy-done, bf16[256,1024]{1,0:T(8,128)(2,1)S(1)} %copy-done.3, bf16[256,1024]{1,0:T(8,128)(2,1)S(1)} %copy-done.2, ...), custom_call_target="tpu_custom_call" | custom-call | flops 10000000000 | bytes 3145728 | tf_op jit(solution)/shard_map/backward_conv/pallas_call | solution.py:195
  25.6 3.2 %all-to-all-done = f32[8,64,128]{2,1,0:T(8,128)S(1)} async-done(((f32[8,64,128]{2,1,0:T(8,128)}), f32[8,64,128]{2,1,0:T(8,128)S(1)}, u32[]{:S(2)}, u32[]{:S(2)}) %all-to-all-start) | async-done | bytes 262176 | tf_op jit(solution)/shard_map/all_to_all | solution.py:222
  28.9 0.7 %broadcast_in_dim.7 = f32[8,64,128]{2,1,0:T(8,128)} broadcast(f32[64,128]{1,0:T(8,128)S(1)} %reduce_sum.27), dimensions={1,2} | broadcast | bytes 294912 | tf_op jit(solution)/shard_map/broadcast_in_dim | solution.py:221
  29.6 6.8 %all-to-all-start.1 = ((f32[8,64,128]{2,1,0:T(8,128)}), f32[8,64,128]{2,1,0:T(8,128)S(1)}, u32[]{:S(2)}, u32[]{:S(2)}) async-start(f32[8,64,128]{2,1,0:T(8,128)} %broadcast_in_dim.7), calls=%async_computation.1 | async-start | bytes 524288 | tf_op jit(solution)/shard_map/all_to_all | solution.py:222
  36.4 2.8 %forward_conv.1 = (bf16[256,1024]{1,0:T(8,128)(2,1)}, bf16[256,1024]{1,0:T(8,128)(2,1)}) custom-call(bf16[256,1024]{1,0:T(8,128)(2,1)S(1)} %copy-done.2, bf16[256,1024]{1,0:T(8,128)(2,1)S(1)} %copy-done.3, bf16[256,1024]{1,0:T(8,128)(2,1)S(1)} %copy-done, bf16[256,1024]{1,0:T(8,128)(2,1)S(1)} %copy-done.1, ...), custom_call_target="tpu_custom_call" | custom-call | flops 10000000000 | bytes 3145728 | tf_op jit(solution)/shard_map/forward_conv/pallas_call | solution.py:195
  39.2 6.6 %all-to-all-done.1 = f32[8,64,128]{2,1,0:T(8,128)S(1)} async-done(((f32[8,64,128]{2,1,0:T(8,128)}), f32[8,64,128]{2,1,0:T(8,128)S(1)}, u32[]{:S(2)}, u32[]{:S(2)}) %all-to-all-start.1) | async-done | bytes 262176 | tf_op jit(solution)/shard_map/all_to_all | solution.py:222
  45.9 19.5 %all_to_all.15.squares_ref = f32[8,1,128]{2,1,0:T(1,128)S(1)} all-to-all(f32[8,1,128]{2,1,0:T(1,128)S(1)} %broadcast_in_dim.8), channel_id=1, replica_groups={{32,33,2,3,4,5,38,39},{0,1,34,35,36,37,6,7},{40,41,10,11,12,13,46,47},{..., dimensions={0} | all-to-all | bytes 8192 | tf_op jit(solution)/shard_map/all_to_all | solution.py:222
  65.3 0.7 %scale.1 = f32[64,128]{1,0:T(8,128)} custom-call(f32[64,128]{1,0:T(8,128)S(1)} %reduce_sum.28.raw_ref, f32[8,1,128]{2,1,0:T(1,128)S(1)} %all_to_all.15.squares_ref), custom_call_target="tpu_custom_call" | custom-call | tf_op jit(solution)/shard_map/scale/pallas_call | solution.py:209
  (7 shorter events, 0.1 us)
Async XLA Ops:
  1.7 9.5 %copy-start.4 = (bf16[64,128]{1,0:T(8,128)(2,1)S(1)}, bf16[64,128]{1,0:T(8,128)(2,1)}, u32[]{:S(2)}) copy-start(bf16[64,128]{1,0:T(8,128)(2,1)} %param.8) | copy-start | bytes 49156
  1.7 9.7 %collective-permute-start = (bf16[128,1024]{1,0:T(8,128)(2,1)S(1)}, bf16[128,1024]{1,0:T(8,128)(2,1)S(1)}, u32[]{:S(2)}, u32[]{:S(2)}) collective-permute-start(bf16[128,1024]{1,0:T(8,128)(2,1)S(1)} %multiply_convert_fusion), channel_id=1, source_target_pairs={{8,0},{16,8},{24,16},{32,24},{40,32},{48,40},{56,48},{64,56},{72,6... | collective-permute-start | bytes 786440 | tf_op jit(solution)/shard_map/ppermute | solution.py:238
  6.6 16.2 %collective-permute-start.1 = (bf16[128,1024]{1,0:T(8,128)(2,1)S(1)}, bf16[128,1024]{1,0:T(8,128)(2,1)S(1)}, u32[]{:S(2)}, u32[]{:S(2)}) collective-permute-start(bf16[128,1024]{1,0:T(8,128)(2,1)S(1)} %get-tuple-element.20.tail_ref), channel_id=1, source_target_pairs={{0,8},{8,16},{16,24},{24,32},{32,40},{40,48},{48,56},{56,64},{64,7... | collective-permute-start | bytes 786440 | tf_op jit(solution)/shard_map/ppermute | solution.py:247
  11.5 11.3 %copy-start.1 = (bf16[256,1024]{1,0:T(8,128)(2,1)S(1)}, bf16[256,1024]{1,0:T(8,128)(2,1)}, u32[]{:S(2)}) copy-start(bf16[256,1024]{1,0:T(8,128)(2,1)} %y_ref.3) | copy-start | bytes 1572868
  11.5 11.3 %copy-start.2 = (bf16[256,1024]{1,0:T(8,128)(2,1)S(1)}, bf16[256,1024]{1,0:T(8,128)(2,1)}, u32[]{:S(2)}) copy-start(bf16[256,1024]{1,0:T(8,128)(2,1)} %a_ref.3) | copy-start | bytes 1572868
  11.5 11.3 %copy-start.3 = (bf16[256,1024]{1,0:T(8,128)(2,1)S(1)}, bf16[256,1024]{1,0:T(8,128)(2,1)}, u32[]{:S(2)}) copy-start(bf16[256,1024]{1,0:T(8,128)(2,1)} %b_ref.3) | copy-start | bytes 1572868
  13.2 9.6 %copy-start = (bf16[256,1024]{1,0:T(8,128)(2,1)S(1)}, bf16[256,1024]{1,0:T(8,128)(2,1)}, u32[]{:S(2)}) copy-start(bf16[256,1024]{1,0:T(8,128)(2,1)} %x_ref.3) | copy-start | bytes 1572868
  13.9 14.9 %all-to-all-start = ((f32[8,64,128]{2,1,0:T(8,128)}), f32[8,64,128]{2,1,0:T(8,128)S(1)}, u32[]{:S(2)}, u32[]{:S(2)}) async-start(f32[8,64,128]{2,1,0:T(8,128)} %broadcast_in_dim.6), calls=%async_computation | async-start | bytes 524288 | tf_op jit(solution)/shard_map/all_to_all | solution.py:222
  29.6 16.3 %all-to-all-start.1 = ((f32[8,64,128]{2,1,0:T(8,128)}), f32[8,64,128]{2,1,0:T(8,128)S(1)}, u32[]{:S(2)}, u32[]{:S(2)}) async-start(f32[8,64,128]{2,1,0:T(8,128)} %broadcast_in_dim.7), calls=%async_computation.1 | async-start | bytes 524288 | tf_op jit(solution)/shard_map/all_to_all | solution.py:222

commit v7 on v6

--- a/solution.py
+++ b/solution.py
@@ -96,9 +96,8 @@
 
 
 def edge_kernel(tail_ref, after_ref, local_ref, raw_ref, rows):
-    @pl.loop(0, tail_ref.shape[1] // LANES, unroll=UNROLL)
-    def _(t):
-        c = lanes_of(t)
+    for t in range(tail_ref.shape[1] // LANES):
+        c = slice(t * LANES, (t + 1) * LANES)
         following = jnp.concatenate([jnp.zeros((K, LANES), jnp.bfloat16), after_ref[:, c]], axis=0)
         correlate(tail_ref[:, c], following, t, rows)
 

time: 66.5 us -> 66.2 us (level)
  no operation moved by 1% of the time
where the time goes in v7:
time: 66.2 us; the launch traced here: 65.7 us
  starting transfers between devices  21.5 us (32%)
  blocking collectives  19.5 us (29%)
  Pallas kernels  11.2 us (17%)
  waiting for transfers between devices  9.85 us (15%)
  local copies, waits for them, and re-layouts  1.64 us (2%)
  other arithmetic  1.24 us (2%)
  between operations  0.8 us (1%)
    all_to_all x1, blocking collectives, spread_over(): lax.all_to_all(spread, axes, split_axis=0, concat_axis=0, tiled=True, axi...  19.5 us
    all_to_all x2, starting transfers between devices, spread_over(): lax.all_to_all(spread, axes, split_axis=0, concat_axis=0, tiled=True, axi...  15.6 us
    all_to_all x2, waiting for transfers between devices, spread_over(): lax.all_to_all(spread, axes, split_axis=0, concat_axis=0, tiled=True, axi...  9.85 us
    pallas_call x2, Pallas kernels, conv(): pl.pallas_call(functools.partial(conv_kernel, causal), in_specs=[VMEM] *...  5.62 us
    ppermute x1, starting transfers between devices, shards(): before = lax.ppermute(tail, CTX, [(i, i + 1) for i in range(owners - 1)])  4.59 us
    pallas_call x1, Pallas kernels, local_filter(): pl.pallas_call(local_kernel, in_specs=[HBM] * 4, out_specs=[VMEM] * 2, ou...  3.55 us
    broadcast_in_dim x3, local copies, waits for them, and re-layouts, spread_over(): spread = jnp.broadcast_to(value[None], (size,) + value.shape)  1.44 us
  transfers between devices with their start and end apart: 4, of which 2 were waited for; matrix products, arithmetic and copies ran while one was open for 1% of the time, Pallas kernels for 16%

profile of v7, /device:TPU:1, one launch (start us, length us, event | category | flops | bytes accessed | tf_op | source)
XLA Modules:
  0.0 65.7 jit_solution(4607862774815713910)
XLA Ops:
  0.6 1.1 %multiply_convert_fusion = bf16[128,1024]{1,0:T(8,128)(2,1)S(1)} fusion(bf16[256,1024]{1,0:T(8,128)(2,1)} %x_ref.3, bf16[256,1024]{1,0:T(8,128)(2,1)} %y_ref.3), kind=kLoop, calls=%fused_computation | loop fusion | flops 524288 | bytes 786432 | tf_op jit(solution)/shard_map/convert_element_type | solution.py:28
  1.7 0.0 copy-start.4
  1.7 1.3 %collective-permute-start = (bf16[128,1024]{1,0:T(8,128)(2,1)S(1)}, bf16[128,1024]{1,0:T(8,128)(2,1)S(1)}, u32[]{:S(2)}, u32[]{:S(2)}) collective-permute-start(bf16[128,1024]{1,0:T(8,128)(2,1)S(1)} %multiply_convert_fusion), channel_id=1, source_target_pairs={{8,0},{16,8},{24,16},{32,24},{40,32},{48,40},{56,48},{64,56},{72,6... | collective-permute-start | bytes 786440 | tf_op jit(solution)/shard_map/ppermute | solution.py:237
  3.0 3.6 %local_filter.1 = (f32[64,128]{1,0:T(8,128)S(1)}, bf16[128,1024]{1,0:T(8,128)(2,1)S(1)}) custom-call(bf16[256,1024]{1,0:T(8,128)(2,1)} %x_ref.3, bf16[256,1024]{1,0:T(8,128)(2,1)} %a_ref.3, bf16[256,1024]{1,0:T(8,128)(2,1)} %b_ref.3, bf16[256,1024]{1,0:T(8,128)(2,1)} %y_ref.3), custom_call_target="tpu_custom_call" | custom-call | flops 3000000000 | bytes 2097152 | tf_op jit(solution)/shard_map/local_filter/pallas_call | solution.py:160
  6.6 4.6 %collective-permute-start.1 = (bf16[128,1024]{1,0:T(8,128)(2,1)S(1)}, bf16[128,1024]{1,0:T(8,128)(2,1)S(1)}, u32[]{:S(2)}, u32[]{:S(2)}) collective-permute-start(bf16[128,1024]{1,0:T(8,128)(2,1)S(1)} %get-tuple-element.20.tail_ref), channel_id=1, source_target_pairs={{0,8},{8,16},{16,24},{24,32},{32,40},{40,48},{48,56},{56,64},{64,7... | collective-permute-start | bytes 786440 | tf_op jit(solution)/shard_map/ppermute | solution.py:246
  11.2 0.0 copy-done.4
  11.2 0.1 rev.3
  11.3 0.1 pad.3.clone
  11.4 0.1 maximum_maximum_fusion.filter_ref
  11.5 0.0 collective-permute-done.after_ref.halo_ref
  11.5 0.0 copy-start.1
  11.5 0.0 copy-start.2
  11.5 0.0 copy-start.3
  11.5 1.3 %edge_filter.1 = f32[64,128]{1,0:T(8,128)S(1)} custom-call(bf16[128,1024]{1,0:T(8,128)(2,1)S(1)} %get-tuple-element.20.tail_ref, bf16[128,1024]{1,0:T(8,128)(2,1)S(1)} %collective-permute-done.after_ref.halo_ref, f32[64,128]{1,0:T(8,128)S(1)} %get-tuple-element.21.local_ref), custom_call_target="tpu_custom_call" | custom-call | flops 1000000000 | bytes 524288 | tf_op jit(solution)/shard_map/edge_filter/pallas_call | solution.py:180
  12.8 0.0 copy-start
  12.9 0.7 %broadcast_in_dim.6 = f32[8,64,128]{2,1,0:T(8,128)} broadcast(f32[64,128]{1,0:T(8,128)S(1)} %edge_filter.1), dimensions={1,2} | broadcast | bytes 294912 | tf_op jit(solution)/shard_map/broadcast_in_dim | solution.py:220
  13.6 8.8 %all-to-all-start = ((f32[8,64,128]{2,1,0:T(8,128)}), f32[8,64,128]{2,1,0:T(8,128)S(1)}, u32[]{:S(2)}, u32[]{:S(2)}) async-start(f32[8,64,128]{2,1,0:T(8,128)} %broadcast_in_dim.6), calls=%async_computation | async-start | bytes 524288 | tf_op jit(solution)/shard_map/all_to_all | solution.py:221
  22.4 0.0 collective-permute-done.1.halo_ref
  22.4 0.0 copy-done.1
  22.4 0.0 copy-done.2
  22.4 0.0 copy-done.3
  22.4 0.0 copy-done
  22.4 2.8 %backward_conv.1 = (bf16[256,1024]{1,0:T(8,128)(2,1)}, bf16[256,1024]{1,0:T(8,128)(2,1)}) custom-call(bf16[256,1024]{1,0:T(8,128)(2,1)S(1)} %copy-done.1, bf16[256,1024]{1,0:T(8,128)(2,1)S(1)} %copy-done, bf16[256,1024]{1,0:T(8,128)(2,1)S(1)} %copy-done.3, bf16[256,1024]{1,0:T(8,128)(2,1)S(1)} %copy-done.2, ...), custom_call_target="tpu_custom_call" | custom-call | flops 10000000000 | bytes 3145728 | tf_op jit(solution)/shard_map/backward_conv/pallas_call | solution.py:194
  25.2 3.2 %all-to-all-done = f32[8,64,128]{2,1,0:T(8,128)S(1)} async-done(((f32[8,64,128]{2,1,0:T(8,128)}), f32[8,64,128]{2,1,0:T(8,128)S(1)}, u32[]{:S(2)}, u32[]{:S(2)}) %all-to-all-start) | async-done | bytes 262176 | tf_op jit(solution)/shard_map/all_to_all | solution.py:221
  28.5 0.7 %broadcast_in_dim.7 = f32[8,64,128]{2,1,0:T(8,128)} broadcast(f32[64,128]{1,0:T(8,128)S(1)} %reduce_sum.27), dimensions={1,2} | broadcast | bytes 294912 | tf_op jit(solution)/shard_map/broadcast_in_dim | solution.py:220
  29.2 6.8 %all-to-all-start.1 = ((f32[8,64,128]{2,1,0:T(8,128)}), f32[8,64,128]{2,1,0:T(8,128)S(1)}, u32[]{:S(2)}, u32[]{:S(2)}) async-start(f32[8,64,128]{2,1,0:T(8,128)} %broadcast_in_dim.7), calls=%async_computation.1 | async-start | bytes 524288 | tf_op jit(solution)/shard_map/all_to_all | solution.py:221
  36.0 2.8 %forward_conv.1 = (bf16[256,1024]{1,0:T(8,128)(2,1)}, bf16[256,1024]{1,0:T(8,128)(2,1)}) custom-call(bf16[256,1024]{1,0:T(8,128)(2,1)S(1)} %copy-done.2, bf16[256,1024]{1,0:T(8,128)(2,1)S(1)} %copy-done.3, bf16[256,1024]{1,0:T(8,128)(2,1)S(1)} %copy-done, bf16[256,1024]{1,0:T(8,128)(2,1)S(1)} %copy-done.1, ...), custom_call_target="tpu_custom_call" | custom-call | flops 10000000000 | bytes 3145728 | tf_op jit(solution)/shard_map/forward_conv/pallas_call | solution.py:194
  38.8 6.7 %all-to-all-done.1 = f32[8,64,128]{2,1,0:T(8,128)S(1)} async-done(((f32[8,64,128]{2,1,0:T(8,128)}), f32[8,64,128]{2,1,0:T(8,128)S(1)}, u32[]{:S(2)}, u32[]{:S(2)}) %all-to-all-start.1) | async-done | bytes 262176 | tf_op jit(solution)/shard_map/all_to_all | solution.py:221
  45.5 19.5 %all_to_all.15.squares_ref = f32[8,1,128]{2,1,0:T(1,128)S(1)} all-to-all(f32[8,1,128]{2,1,0:T(1,128)S(1)} %broadcast_in_dim.8), channel_id=1, replica_groups={{32,33,2,3,4,5,38,39},{0,1,34,35,36,37,6,7},{40,41,10,11,12,13,46,47},{..., dimensions={0} | all-to-all | bytes 8192 | tf_op jit(solution)/shard_map/all_to_all | solution.py:221
  65.0 0.7 %scale.1 = f32[64,128]{1,0:T(8,128)} custom-call(f32[64,128]{1,0:T(8,128)S(1)} %reduce_sum.28.raw_ref, f32[8,1,128]{2,1,0:T(1,128)S(1)} %all_to_all.15.squares_ref), custom_call_target="tpu_custom_call" | custom-call | tf_op jit(solution)/shard_map/scale/pallas_call | solution.py:208
  (7 shorter events, 0.1 us)
Async XLA Ops:
  1.7 9.5 %copy-start.4 = (bf16[64,128]{1,0:T(8,128)(2,1)S(1)}, bf16[64,128]{1,0:T(8,128)(2,1)}, u32[]{:S(2)}) copy-start(bf16[64,128]{1,0:T(8,128)(2,1)} %param.8) | copy-start | bytes 49156
  1.7 9.7 %collective-permute-start = (bf16[128,1024]{1,0:T(8,128)(2,1)S(1)}, bf16[128,1024]{1,0:T(8,128)(2,1)S(1)}, u32[]{:S(2)}, u32[]{:S(2)}) collective-permute-start(bf16[128,1024]{1,0:T(8,128)(2,1)S(1)} %multiply_convert_fusion), channel_id=1, source_target_pairs={{8,0},{16,8},{24,16},{32,24},{40,32},{48,40},{56,48},{64,56},{72,6... | collective-permute-start | bytes 786440 | tf_op jit(solution)/shard_map/ppermute | solution.py:237
  6.6 15.8 %collective-permute-start.1 = (bf16[128,1024]{1,0:T(8,128)(2,1)S(1)}, bf16[128,1024]{1,0:T(8,128)(2,1)S(1)}, u32[]{:S(2)}, u32[]{:S(2)}) collective-permute-start(bf16[128,1024]{1,0:T(8,128)(2,1)S(1)} %get-tuple-element.20.tail_ref), channel_id=1, source_target_pairs={{0,8},{8,16},{16,24},{24,32},{32,40},{40,48},{48,56},{56,64},{64,7... | collective-permute-start | bytes 786440 | tf_op jit(solution)/shard_map/ppermute | solution.py:246
  11.5 10.9 %copy-start.1 = (bf16[256,1024]{1,0:T(8,128)(2,1)S(1)}, bf16[256,1024]{1,0:T(8,128)(2,1)}, u32[]{:S(2)}) copy-start(bf16[256,1024]{1,0:T(8,128)(2,1)} %y_ref.3) | copy-start | bytes 1572868
  11.5 10.9 %copy-start.2 = (bf16[256,1024]{1,0:T(8,128)(2,1)S(1)}, bf16[256,1024]{1,0:T(8,128)(2,1)}, u32[]{:S(2)}) copy-start(bf16[256,1024]{1,0:T(8,128)(2,1)} %a_ref.3) | copy-start | bytes 1572868
  11.5 10.9 %copy-start.3 = (bf16[256,1024]{1,0:T(8,128)(2,1)S(1)}, bf16[256,1024]{1,0:T(8,128)(2,1)}, u32[]{:S(2)}) copy-start(bf16[256,1024]{1,0:T(8,128)(2,1)} %b_ref.3) | copy-start | bytes 1572868
  12.8 9.6 %copy-start = (bf16[256,1024]{1,0:T(8,128)(2,1)S(1)}, bf16[256,1024]{1,0:T(8,128)(2,1)}, u32[]{:S(2)}) copy-start(bf16[256,1024]{1,0:T(8,128)(2,1)} %x_ref.3) | copy-start | bytes 1572868
  13.6 14.9 %all-to-all-start = ((f32[8,64,128]{2,1,0:T(8,128)}), f32[8,64,128]{2,1,0:T(8,128)S(1)}, u32[]{:S(2)}, u32[]{:S(2)}) async-start(f32[8,64,128]{2,1,0:T(8,128)} %broadcast_in_dim.6), calls=%async_computation | async-start | bytes 524288 | tf_op jit(solution)/shard_map/all_to_all | solution.py:221
  29.2 16.3 %all-to-all-start.1 = ((f32[8,64,128]{2,1,0:T(8,128)}), f32[8,64,128]{2,1,0:T(8,128)S(1)}, u32[]{:S(2)}, u32[]{:S(2)}) async-start(f32[8,64,128]{2,1,0:T(8,128)} %broadcast_in_dim.7), calls=%async_computation.1 | async-start | bytes 524288 | tf_op jit(solution)/shard_map/all_to_all | solution.py:221

commit v8 on v7

--- a/solution.py
+++ b/solution.py
@@ -14,8 +14,8 @@
 FB = 32
 W = 2 * K
 LANES = 128
-UNROLL = 4
 LIMIT = 8 << 20
+CHUNK = 4
 LOCAL_LIMIT = 107 << 19
 TILE_GROUPS = LANES // G
 CTX = ("y", "zl", "x")
@@ -69,28 +69,26 @@
 
 def local_kernel(q_hbm, k_hbm, v_hbm, go_hbm, raw_ref, tail_ref, q_buf, k_buf, v_buf, go_buf, rows, sems):
     tokens, channels = q_buf.shape
-    chunk = UNROLL * LANES
-
-    def copies_of(i):
-        c = pl.ds(pl.multiple_of(i * chunk, chunk), chunk)
-        pairs = ((k_hbm, k_buf), (v_hbm, v_buf), (go_hbm, go_buf), (q_hbm, q_buf))
-        return [pltpu.make_async_copy(src.at[:, c], dst.at[:, c], sems.at[n, i]) for n, (src, dst) in enumerate(pairs)]
-
-    @pl.loop(0, channels // chunk)
-    def _(i):
-        for copy in copies_of(i):
+    chunk = CHUNK * LANES
+    pairs = ((k_hbm, k_buf), (v_hbm, v_buf), (go_hbm, go_buf), (q_hbm, q_buf))
+    copies = [
+        [
+            pltpu.make_async_copy(src.at[:, i : i + chunk], dst.at[:, i : i + chunk], sems.at[n, i // chunk])
+            for n, (src, dst) in enumerate(pairs)
+        ]
+        for i in range(0, channels, chunk)
+    ]
+    for group in copies:
+        for copy in group:
             copy.start()
-
-    @pl.loop(0, channels // chunk)
-    def _(i):
-        for copy in copies_of(i):
-            copy.wait()
-        for u in range(UNROLL):
-            t = i * UNROLL + u
-            c = lanes_of(t)
-            product = product_of(k_buf[:, c], v_buf[:, c])
-            tail_ref[:, c] = product[tokens - K :]
-            correlate(product, product_of(go_buf[:, c], q_buf[:, c]), t, rows)
+    for t in range(channels // LANES):
+        if t % CHUNK == 0:
+            for copy in copies[t // CHUNK]:
+                copy.wait()
+        c = slice(t * LANES, (t + 1) * LANES)
+        product = product_of(k_buf[:, c], v_buf[:, c])
+        tail_ref[:, c] = product[tokens - K :]
+        correlate(product, product_of(go_buf[:, c], q_buf[:, c]), t, rows)
 
     raw_ref[...] = fold(rows)
 
@@ -168,7 +166,7 @@
         scratch_shapes=[pltpu.VMEM(q.shape, jnp.bfloat16)] * 4
         + [
             pltpu.VMEM((slab_groups * 8, W), jnp.float32),
-            pltpu.SemaphoreType.DMA((4, q.shape[1] // (UNROLL * LANES))),
+            pltpu.SemaphoreType.DMA((4, q.shape[1] // (CHUNK * LANES))),
         ],
         cost_estimate=pl.CostEstimate(flops=3 * 10**9, bytes_accessed=2**21, transcendentals=0),
         compiler_params=pltpu.CompilerParams(vmem_limit_bytes=LOCAL_LIMIT),
@@ -238,6 +236,7 @@
     local, tail = local_filter(queries, key_feats, value_feats, grad_out, slab_groups)
     raw = edge_filter(tail, after, local)
 
+    filters, _ = lax.optimization_barrier((filters, raw))
     filt = filters.astype(jnp.float32)
     zeros = jnp.zeros((slab_groups, W - K), jnp.float32)
     backward_rows = jnp.concatenate([filt, zeros], axis=1)

time: 66.2 us -> 66.2 us (level)
  transfers between devices with their start and end apart: 4 -> 4, of which waited for: 2 -> 2; matrix products, arithmetic and copies ran while one was open for 1% -> 1% of each run, Pallas kernels for 16% -> 15%
where the time goes in v8:
time: 66.2 us; the launch traced here: 65.7 us
  starting transfers between devices  21.9 us (33%)
  blocking collectives  19.6 us (30%)
  Pallas kernels  10.9 us (16%)
  waiting for transfers between devices  9.69 us (15%)
  local copies, waits for them, and re-layouts  1.64 us (2%)
  other arithmetic  1.25 us (2%)
  between operations  0.79 us (1%)
    all_to_all x1, blocking collectives, spread_over(): lax.all_to_all(spread, axes, split_axis=0, concat_axis=0, tiled=True, axi...  19.6 us
    all_to_all x2, starting transfers between devices, spread_over(): lax.all_to_all(spread, axes, split_axis=0, concat_axis=0, tiled=True, axi...  16 us
    all_to_all x2, waiting for transfers between devices, spread_over(): lax.all_to_all(spread, axes, split_axis=0, concat_axis=0, tiled=True, axi...  9.68 us
    pallas_call x2, Pallas kernels, conv(): pl.pallas_call(functools.partial(conv_kernel, causal), in_specs=[VMEM] *...  5.59 us
    ppermute x1, starting transfers between devices, shards(): before = lax.ppermute(tail, CTX, [(i, i + 1) for i in range(owners - 1)])  4.59 us
    pallas_call x1, Pallas kernels, local_filter(): pl.pallas_call(local_kernel, in_specs=[HBM] * 4, out_specs=[VMEM] * 2, ou...  3.26 us
    broadcast_in_dim x3, local copies, waits for them, and re-layouts, spread_over(): spread = jnp.broadcast_to(value[None], (size,) + value.shape)  1.44 us
    pallas_call x1, Pallas kernels, edge_filter(): pl.pallas_call(edge_kernel, in_specs=[VMEM] * 3, out_specs=VMEM, out_shap...  1.33 us
  transfers between devices with their start and end apart: 4, of which 2 were waited for; matrix products, arithmetic and copies ran while one was open for 1% of the time, Pallas kernels for 15%

profile of v8, /device:TPU:1, one launch (start us, length us, event | category | flops | bytes accessed | tf_op | source)
XLA Modules:
  0.0 65.7 jit_solution(4494814679279265520)
XLA Ops:
  0.6 1.1 %multiply_convert_fusion = bf16[128,1024]{1,0:T(8,128)(2,1)S(1)} fusion(bf16[256,1024]{1,0:T(8,128)(2,1)} %x_ref.3, bf16[256,1024]{1,0:T(8,128)(2,1)} %y_ref.3), kind=kLoop, calls=%fused_computation | loop fusion | flops 524288 | bytes 786432 | tf_op jit(solution)/shard_map/convert_element_type | solution.py:28
  1.7 1.3 %collective-permute-start = (bf16[128,1024]{1,0:T(8,128)(2,1)S(1)}, bf16[128,1024]{1,0:T(8,128)(2,1)S(1)}, u32[]{:S(2)}, u32[]{:S(2)}) collective-permute-start(bf16[128,1024]{1,0:T(8,128)(2,1)S(1)} %multiply_convert_fusion), channel_id=1, source_target_pairs={{8,0},{16,8},{24,16},{32,24},{40,32},{48,40},{56,48},{64,56},{72,6... | collective-permute-start | bytes 786440 | tf_op jit(solution)/shard_map/ppermute | solution.py:235
  3.0 3.3 %local_filter.1 = (f32[64,128]{1,0:T(8,128)S(1)}, bf16[128,1024]{1,0:T(8,128)(2,1)S(1)}) custom-call(bf16[256,1024]{1,0:T(8,128)(2,1)} %x_ref.3, bf16[256,1024]{1,0:T(8,128)(2,1)} %a_ref.3, bf16[256,1024]{1,0:T(8,128)(2,1)} %b_ref.3, bf16[256,1024]{1,0:T(8,128)(2,1)} %y_ref.3), custom_call_target="tpu_custom_call" | custom-call | flops 3000000000 | bytes 2097152 | tf_op jit(solution)/shard_map/local_filter/pallas_call | solution.py:158
  6.3 4.6 %collective-permute-start.1 = (bf16[128,1024]{1,0:T(8,128)(2,1)S(1)}, bf16[128,1024]{1,0:T(8,128)(2,1)S(1)}, u32[]{:S(2)}, u32[]{:S(2)}) collective-permute-start(bf16[128,1024]{1,0:T(8,128)(2,1)S(1)} %get-tuple-element.21.tail_ref), channel_id=1, source_target_pairs={{0,8},{8,16},{16,24},{24,32},{32,40},{40,48},{48,56},{56,64},{64,7... | collective-permute-start | bytes 786440 | tf_op jit(solution)/shard_map/ppermute | solution.py:245
  10.9 0.1 pad.3.clone
  11.0 0.0 collective-permute-done.after_ref.halo_ref
  11.0 0.0 copy-start.4
  11.0 0.0 copy-start.1
  11.0 0.0 copy-start.2
  11.0 0.0 copy-start.3
  11.0 1.3 %edge_filter.1 = f32[64,128]{1,0:T(8,128)S(1)} custom-call(bf16[128,1024]{1,0:T(8,128)(2,1)S(1)} %get-tuple-element.21.tail_ref, bf16[128,1024]{1,0:T(8,128)(2,1)S(1)} %collective-permute-done.after_ref.halo_ref, f32[64,128]{1,0:T(8,128)S(1)} %get-tuple-element.22.local_ref), custom_call_target="tpu_custom_call" | custom-call | flops 1000000000 | bytes 524288 | tf_op jit(solution)/shard_map/edge_filter/pallas_call | solution.py:178
  12.4 0.0 copy-done.4
  12.4 0.0 copy-start
  12.4 0.7 %broadcast_in_dim.6 = f32[8,64,128]{2,1,0:T(8,128)} broadcast(f32[64,128]{1,0:T(8,128)S(1)} %edge_filter.1), dimensions={1,2} | broadcast | bytes 294912 | tf_op jit(solution)/shard_map/broadcast_in_dim | solution.py:218
  13.1 9.2 %all-to-all-start = ((f32[8,64,128]{2,1,0:T(8,128)}), f32[8,64,128]{2,1,0:T(8,128)S(1)}, u32[]{:S(2)}, u32[]{:S(2)}) async-start(f32[8,64,128]{2,1,0:T(8,128)} %broadcast_in_dim.6), calls=%async_computation | async-start | bytes 524288 | tf_op jit(solution)/shard_map/all_to_all | solution.py:219
  22.3 0.0 collective-permute-done.1.halo_ref
  22.3 0.0 copy-done.1
  22.3 0.0 copy-done.2
  22.3 0.0 copy-done.3
  22.3 0.0 copy-done
  22.3 2.8 %backward_conv.1 = (bf16[256,1024]{1,0:T(8,128)(2,1)}, bf16[256,1024]{1,0:T(8,128)(2,1)}) custom-call(bf16[256,1024]{1,0:T(8,128)(2,1)S(1)} %copy-done.1, bf16[256,1024]{1,0:T(8,128)(2,1)S(1)} %copy-done, bf16[256,1024]{1,0:T(8,128)(2,1)S(1)} %copy-done.3, bf16[256,1024]{1,0:T(8,128)(2,1)S(1)} %copy-done.2, ...), custom_call_target="tpu_custom_call" | custom-call | flops 10000000000 | bytes 3145728 | tf_op jit(solution)/shard_map/backward_conv/pallas_call | solution.py:192
  25.2 0.1 rev.3
  25.2 0.1 maximum_maximum_fusion.filter_ref
  25.3 3.0 %all-to-all-done = f32[8,64,128]{2,1,0:T(8,128)S(1)} async-done(((f32[8,64,128]{2,1,0:T(8,128)}), f32[8,64,128]{2,1,0:T(8,128)S(1)}, u32[]{:S(2)}, u32[]{:S(2)}) %all-to-all-start) | async-done | bytes 262176 | tf_op jit(solution)/shard_map/all_to_all | solution.py:219
  28.4 0.7 %broadcast_in_dim.7 = f32[8,64,128]{2,1,0:T(8,128)} broadcast(f32[64,128]{1,0:T(8,128)S(1)} %reduce_sum.27), dimensions={1,2} | broadcast | bytes 294912 | tf_op jit(solution)/shard_map/broadcast_in_dim | solution.py:218
  29.1 6.8 %all-to-all-start.1 = ((f32[8,64,128]{2,1,0:T(8,128)}), f32[8,64,128]{2,1,0:T(8,128)S(1)}, u32[]{:S(2)}, u32[]{:S(2)}) async-start(f32[8,64,128]{2,1,0:T(8,128)} %broadcast_in_dim.7), calls=%async_computation.1 | async-start | bytes 524288 | tf_op jit(solution)/shard_map/all_to_all | solution.py:219
  35.9 2.8 %forward_conv.1 = (bf16[256,1024]{1,0:T(8,128)(2,1)}, bf16[256,1024]{1,0:T(8,128)(2,1)}) custom-call(bf16[256,1024]{1,0:T(8,128)(2,1)S(1)} %copy-done.2, bf16[256,1024]{1,0:T(8,128)(2,1)S(1)} %copy-done.3, bf16[256,1024]{1,0:T(8,128)(2,1)S(1)} %copy-done, bf16[256,1024]{1,0:T(8,128)(2,1)S(1)} %copy-done.1, ...), custom_call_target="tpu_custom_call" | custom-call | flops 10000000000 | bytes 3145728 | tf_op jit(solution)/shard_map/forward_conv/pallas_call | solution.py:192
  38.7 6.6 %all-to-all-done.1 = f32[8,64,128]{2,1,0:T(8,128)S(1)} async-done(((f32[8,64,128]{2,1,0:T(8,128)}), f32[8,64,128]{2,1,0:T(8,128)S(1)}, u32[]{:S(2)}, u32[]{:S(2)}) %all-to-all-start.1) | async-done | bytes 262176 | tf_op jit(solution)/shard_map/all_to_all | solution.py:219
  45.4 19.6 %all_to_all.15.squares_ref = f32[8,1,128]{2,1,0:T(1,128)S(1)} all-to-all(f32[8,1,128]{2,1,0:T(1,128)S(1)} %broadcast_in_dim.8), channel_id=1, replica_groups={{32,33,2,3,4,5,38,39},{0,1,34,35,36,37,6,7},{40,41,10,11,12,13,46,47},{..., dimensions={0} | all-to-all | bytes 8192 | tf_op jit(solution)/shard_map/all_to_all | solution.py:219
  65.0 0.7 %scale.1 = f32[64,128]{1,0:T(8,128)} custom-call(f32[64,128]{1,0:T(8,128)S(1)} %reduce_sum.28.raw_ref, f32[8,1,128]{2,1,0:T(1,128)S(1)} %all_to_all.15.squares_ref), custom_call_target="tpu_custom_call" | custom-call | tf_op jit(solution)/shard_map/scale/pallas_call | solution.py:206
  (7 shorter events, 0.1 us)
Async XLA Ops:
  1.7 9.3 %collective-permute-start = (bf16[128,1024]{1,0:T(8,128)(2,1)S(1)}, bf16[128,1024]{1,0:T(8,128)(2,1)S(1)}, u32[]{:S(2)}, u32[]{:S(2)}) collective-permute-start(bf16[128,1024]{1,0:T(8,128)(2,1)S(1)} %multiply_convert_fusion), channel_id=1, source_target_pairs={{8,0},{16,8},{24,16},{32,24},{40,32},{48,40},{56,48},{64,56},{72,6... | collective-permute-start | bytes 786440 | tf_op jit(solution)/shard_map/ppermute | solution.py:235
  6.3 16.0 %collective-permute-start.1 = (bf16[128,1024]{1,0:T(8,128)(2,1)S(1)}, bf16[128,1024]{1,0:T(8,128)(2,1)S(1)}, u32[]{:S(2)}, u32[]{:S(2)}) collective-permute-start(bf16[128,1024]{1,0:T(8,128)(2,1)S(1)} %get-tuple-element.21.tail_ref), channel_id=1, source_target_pairs={{0,8},{8,16},{16,24},{24,32},{32,40},{40,48},{48,56},{56,64},{64,7... | collective-permute-start | bytes 786440 | tf_op jit(solution)/shard_map/ppermute | solution.py:245
  11.0 1.4 %copy-start.4 = (bf16[64,128]{1,0:T(8,128)(2,1)S(1)}, bf16[64,128]{1,0:T(8,128)(2,1)}, u32[]{:S(2)}) copy-start(bf16[64,128]{1,0:T(8,128)(2,1)} %param.8) | copy-start | bytes 49156
  11.0 11.3 %copy-start.1 = (bf16[256,1024]{1,0:T(8,128)(2,1)S(1)}, bf16[256,1024]{1,0:T(8,128)(2,1)}, u32[]{:S(2)}) copy-start(bf16[256,1024]{1,0:T(8,128)(2,1)} %y_ref.3) | copy-start | bytes 1572868
  11.0 11.3 %copy-start.2 = (bf16[256,1024]{1,0:T(8,128)(2,1)S(1)}, bf16[256,1024]{1,0:T(8,128)(2,1)}, u32[]{:S(2)}) copy-start(bf16[256,1024]{1,0:T(8,128)(2,1)} %a_ref.3) | copy-start | bytes 1572868
  11.0 11.3 %copy-start.3 = (bf16[256,1024]{1,0:T(8,128)(2,1)S(1)}, bf16[256,1024]{1,0:T(8,128)(2,1)}, u32[]{:S(2)}) copy-start(bf16[256,1024]{1,0:T(8,128)(2,1)} %b_ref.3) | copy-start | bytes 1572868
  12.4 10.0 %copy-start = (bf16[256,1024]{1,0:T(8,128)(2,1)S(1)}, bf16[256,1024]{1,0:T(8,128)(2,1)}, u32[]{:S(2)}) copy-start(bf16[256,1024]{1,0:T(8,128)(2,1)} %x_ref.3) | copy-start | bytes 1572868
  13.1 15.2 %all-to-all-start = ((f32[8,64,128]{2,1,0:T(8,128)}), f32[8,64,128]{2,1,0:T(8,128)S(1)}, u32[]{:S(2)}, u32[]{:S(2)}) async-start(f32[8,64,128]{2,1,0:T(8,128)} %broadcast_in_dim.6), calls=%async_computation | async-start | bytes 524288 | tf_op jit(solution)/shard_map/all_to_all | solution.py:219
  29.1 16.3 %all-to-all-start.1 = ((f32[8,64,128]{2,1,0:T(8,128)}), f32[8,64,128]{2,1,0:T(8,128)S(1)}, u32[]{:S(2)}, u32[]{:S(2)}) async-start(f32[8,64,128]{2,1,0:T(8,128)} %broadcast_in_dim.7), calls=%async_computation.1 | async-start | bytes 524288 | tf_op jit(solution)/shard_map/all_to_all | solution.py:219
